TPU v7x, 32 devices: a whole 2x2x4 slice. The times are simulated.
32 devices in a mesh: dp: 4 (over z), row: 4 (over y, x), col: 2 (over core).
Axes of the slice: x: 2, y: 2, z: 4, core: 2. Of those that a mesh axis runs over, the one named last changes fastest.
Arguments:
- block_input: bfloat16 [4096, 1024], P(('dp', 'row'), 'col'), may hold values from -20 to 20
- output_grad: bfloat16 [4096, 1024], P(('dp', 'row'), 'col'), may hold values from -6 to 6
- document_ids: int32 [4, 1024], P('dp'), may hold values from 0 to 3, never falling along the last dimension, each value on 1 to 512 neighbouring positions
- mixer_gain: bfloat16 [1024], P('col'), may hold values from 0.25 to 1.75
- mamba_gate: bfloat16 [1024, 1536], P('col', 'row'), may hold values from -0.1875 to 0.1875
- mamba_input: bfloat16 [1024, 1536], P('col', 'row'), may hold values from -0.1875 to 0.1875
- mamba_step: bfloat16 [1024, 24], P('col', 'row'), may hold values from -0.1875 to 0.1875
- query_weight: bfloat16 [1024, 512], P('col', 'row'), may hold values from -0.1875 to 0.1875
- key_weight: bfloat16 [1024, 128], P('col'), may hold values from -0.1875 to 0.1875
- value_weight: bfloat16 [1024, 128], P('col'), may hold values from -0.1875 to 0.1875
- state_weight: bfloat16 [1024, 256], P('col'), may hold values from -0.1875 to 0.1875
- input_filter: bfloat16 [1536, 4], P(('row', 'col')), may hold values from -3 to 3
- input_shift: bfloat16 [1536], P(('row', 'col')), may hold values from -0.5 to 0.5
- state_filter: bfloat16 [256, 4], replicated, may hold values from -3 to 3
- state_shift: bfloat16 [256], replicated, may hold values from -0.5 to 0.5
- step_bias: bfloat16 [24], P(('row', 'col')), may hold values from -5 to -1
- decay_log: bfloat16 [24], P(('row', 'col')), may hold values from 0 to 2.6875
- skip_gain: bfloat16 [24], P(('row', 'col')), may hold values from 0.5 to 1.5
- mixer_out: bfloat16 [2048, 1024], P('row', 'col'), may hold values from -4 to 4
- feed_gain: bfloat16 [1024], P('col'), may hold values from 0.25 to 1.75
- feed_gate: bfloat16 [1024, 2048], P('col', 'row'), may hold values from -0.1875 to 0.1875
- feed_up: bfloat16 [1024, 2048], P('col', 'row'), may hold values from -0.1875 to 0.1875
- feed_down: bfloat16 [2048, 1024], P('row', 'col'), may hold values from -0.125 to 0.125
Outputs:
- block_output: float32 [4096, 1024], P(('dp', 'row'), 'col')
- input_grad: float32 [4096, 1024], P(('dp', 'row'), 'col')
- mixer_gain_gradient: float32 [1024], P('col')
- mamba_gate_gradient: float32 [1024, 1536], P('col', 'row')
- mamba_input_gradient: float32 [1024, 1536], P('col', 'row')
- mamba_step_gradient: float32 [1024, 24], P('col', 'row')
- query_weight_gradient: float32 [1024, 512], P('col', 'row')
- key_weight_gradient: float32 [1024, 128], P('col')
- value_weight_gradient: float32 [1024, 128], P('col')
- state_weight_gradient: float32 [1024, 256], P('col')
- input_filter_gradient: float32 [1536, 4], P(('row', 'col'))
- input_shift_gradient: float32 [1536], P(('row', 'col'))
- state_filter_gradient: float32 [256, 4], replicated
- state_shift_gradient: float32 [256], replicated
- step_bias_gradient: float32 [24], P(('row', 'col'))
- decay_log_gradient: float32 [24], P(('row', 'col'))
- skip_gain_gradient: float32 [24], P(('row', 'col'))
- mixer_out_gradient: float32 [2048, 1024], P('row', 'col')
- feed_gain_gradient: float32 [1024], P('col')
- feed_gate_gradient: float32 [1024, 2048], P('col', 'row')
- feed_up_gradient: float32 [1024, 2048], P('col', 'row')
- feed_down_gradient: float32 [2048, 1024], P('row', 'col')
Inputs may be any that keep to these rules, and one draw needn't show every extreme that they name: `document_ids`: along a sequence the document number never falls; each document is a run of one to half of 1024 tokens, and one run in each sequence is exactly that long.
All inputs are finite; a program needn't handle non-finite values.
Results may differ from a plain program's by a relative error of at most 0.039.
Values may be sent and summed in bfloat16 or wider, within the bound.
No kernel may reach another device: no remote copies, remote signals or barrier semaphores. Data moves between devices by JAX's collectives and lax.ppermute only.
A program may use at most 128 MiB of HBM per device.

v0:
```python
from functools import partial

import jax
import jax.numpy as jnp
from jax import lax
from jax.sharding import PartitionSpec as P

D = 1024
HD = 64
QH = 8
KVH = 2
STRETCH = 256


EPS = 1e-05
ROPE_BASE = 100000000000.0
HIGH = lax.Precision.HIGHEST


def as_sent(x):

    def short(part):
        return part.astype(jnp.bfloat16) if part.dtype == jnp.float32 else part

    return jax.tree.map(short, x)


def product(left, right):
    return jnp.dot(left, right, preferred_element_type=jnp.float32)


def against(left, right):
    return lax.dot_general(
        left, right, (((1,), (1,)), ((), ())), preferred_element_type=jnp.float32
    )


def outer(left, right):
    return lax.dot_general(
        left, right, (((0,), (0,)), ((), ())), preferred_element_type=jnp.float32
    )


def exact_against(left, right):
    return lax.dot_general(
        left, right, (((1,), (1,)), ((), ())), precision=HIGH, preferred_element_type=jnp.float32
    )


def exact_outer(left, right):
    return lax.dot_general(
        left, right, (((0,), (0,)), ((), ())), precision=HIGH, preferred_element_type=jnp.float32
    )


def rounded(values):
    return lax.optimization_barrier(values.astype(jnp.bfloat16)).astype(jnp.float32)


def take_rows(values, start, count):
    return lax.dynamic_slice_in_dim(values, start, count, 0)


def col_total(values):
    return lax.psum(values, "col")


def row_tokens(values):
    return lax.all_gather(values, "row", axis=0, tiled=True)


def col_features(values):
    return lax.all_gather(values, "col", axis=1, tiled=True)


def feature_grads(values):
    return lax.psum_scatter(
        values.astype(jnp.bfloat16), "col", scatter_dimension=1, tiled=True
    ).astype(jnp.float32)


def row_out(term, rows):
    return lax.psum_scatter(
        term(jnp.int32(0), lax.axis_size("row") * rows).astype(jnp.bfloat16),
        "row",
        scatter_dimension=0,
        tiled=True,
    ).astype(jnp.float32)


def feed_sum(gate_wgrad, upper_wgrad, down_wgrad):
    return (
        lax.psum(gate_wgrad.astype(jnp.bfloat16), "dp").astype(jnp.float32),
        lax.psum(upper_wgrad.astype(jnp.bfloat16), "dp").astype(jnp.float32),
        lax.psum(down_wgrad.astype(jnp.bfloat16), "dp").astype(jnp.float32),
    )


def norm_forward(residual, gain):
    total = col_total(jnp.sum(residual * residual, axis=1))
    inverse = lax.rsqrt(total / D + EPS)
    return ((residual * inverse[:, None] * gain).astype(jnp.bfloat16), inverse)


def norm_backward(residual, inverse, gain, upstream):
    scaled = upstream * gain
    inner = col_total(jnp.sum(scaled * residual, axis=1))
    input_part = inverse[:, None] * scaled - residual * (inverse**3 * inner / D)[:, None]
    gain_part = jnp.sum(upstream * residual * inverse[:, None], axis=0)
    return (input_part, gain_part)


def causal_filter(values, weight, shift):
    taps = weight.shape[1]
    length = values.shape[1]
    padded = jnp.pad(values, ((0, 0), (taps - 1, 0), (0, 0)))
    result = shift + padded[:, 0:length] * weight[:, 0]
    for index in range(1, taps):
        result = result + padded[:, index : index + length] * weight[:, index]
    return result


def rotate(values, sign):
    length = values.shape[-3]
    width = values.shape[-1]
    half = width // 2
    place = jnp.arange(length).astype(values.dtype)
    rates = ROPE_BASE ** (-2.0 * jnp.arange(half).astype(values.dtype) / width)
    angle = place[:, None] * rates[None, :]
    cosine = jnp.cos(angle)[:, None, :]
    sine = sign * jnp.sin(angle)[:, None, :]
    first = values[..., :half]
    second = values[..., half:]
    return jnp.concatenate(
        [first * cosine - second * sine, second * cosine + first * sine], axis=-1
    )


def ssd_scan(inputs, steps, rates, inject, readout, segment):
    length, heads, width = inputs.shape
    states = inject.shape[1]
    blocks = length // STRETCH
    place = jnp.arange(STRETCH)
    before = place[:, None] >= place[None, :]

    def advance(carry, piece):
        state, last_doc = carry
        part_in, part_step, part_inject, part_read, part_doc = piece
        logs = jnp.cumsum(part_step * rates, axis=0)
        logs_heads = logs.T
        step_heads = part_step.T
        allowed = ((part_doc[:, None] == part_doc[None, :]) & before)[None, :, :]
        spread = jnp.where(allowed, logs_heads[:, :, None] - logs_heads[:, None, :], 0.0)
        decay = jnp.where(allowed, jnp.exp(spread), 0.0)
        intersection = jnp.dot(part_read, part_inject.T, precision=HIGH)
        mixing = intersection[None, :, :] * decay * step_heads[:, None, :]
        inner = jnp.einsum("hts,shp->thp", mixing, part_in, precision=HIGH)
        keep = (part_doc == last_doc).astype(part_in.dtype)
        carried = (
            jnp.einsum("tn,hnp->thp", part_read, state, precision=HIGH)
            * (jnp.exp(logs) * keep[:, None])[:, :, None]
        )
        end_doc = part_doc[STRETCH - 1]
        tail = (part_doc == end_doc).astype(part_in.dtype)
        towards = jnp.exp(logs[STRETCH - 1][None, :] - logs) * tail[:, None] * part_step
        going = jnp.exp(logs[STRETCH - 1]) * (end_doc == last_doc).astype(part_in.dtype)
        state = state * going[:, None, None] + jnp.einsum(
            "sh,sn,shp->hnp", towards, part_inject, part_in, precision=HIGH
        )
        return ((state, end_doc), inner + carried)

    def split(values):
        return values.reshape((blocks, STRETCH) + values.shape[1:])

    start = (jnp.zeros((heads, states, width), inputs.dtype), jnp.int32(-1))
    final, outputs = lax.scan(
        jax.checkpoint(advance),
        start,
        (split(inputs), split(steps), split(inject), split(readout), split(segment)),
    )
    return outputs.reshape(length, heads, width)


def mamba_piece(
    segment,
    input_values,
    gate_values,
    step_values,
    state_conv,
    filter_weight,
    filter_shift,
    step_bias,
    decay_log,
    skip_gain,
):
    sequences, length = segment.shape
    heads = step_values.shape[1]
    channels = input_values.shape[1]
    width = channels // heads
    states = state_conv.shape[1] // 2
    filtered = jax.nn.silu(
        causal_filter(
            input_values.reshape(sequences, length, channels), filter_weight, filter_shift
        )
    )
    filtered = filtered.reshape(sequences, length, heads, width)
    steps = jax.nn.softplus(step_values + step_bias).reshape(sequences, length, heads)
    rates = -jnp.exp(decay_log)
    shared = state_conv.reshape(sequences, length, 2 * states)
    mixed = jax.vmap(ssd_scan, in_axes=(0, 0, None, 0, 0, 0))(
        filtered, steps, rates, shared[..., :states], shared[..., states:], segment
    )
    mixed = mixed + skip_gain[:, None] * filtered
    return mixed.reshape(sequences * length, channels) * jax.nn.silu(gate_values)


def state_piece(sequences, state_raw, filter_weight, filter_shift):
    total, width = state_raw.shape
    filtered = causal_filter(
        state_raw.reshape(sequences, total // sequences, width), filter_weight, filter_shift
    )
    return jax.nn.silu(filtered).reshape(total, width)


def attend_forward(item):
    query, keys, values, segment = item
    length, width = query.shape
    block = min(512, length)
    scale = width ** (-0.5)
    place = jnp.arange(length)
    outputs = []
    totals = []
    for first in range(0, length, block):
        allowed = (segment[first : first + block, None] == segment[None, :]) & (
            place[first : first + block, None] >= place[None, :]
        )
        scores = jnp.where(allowed, against(query[first : first + block], keys) * scale, -1e30)
        peak = jnp.max(scores, axis=1, keepdims=True)
        weights = jnp.exp(scores - peak)
        denominator = jnp.sum(weights, axis=1, keepdims=True)
        probs = (weights / denominator).astype(jnp.bfloat16)
        outputs.append(product(probs, values))
        totals.append(peak[:, 0] + jnp.log(denominator[:, 0]))
    return (jnp.concatenate(outputs, axis=0), jnp.concatenate(totals, axis=0))


def attend_backward(item):
    query, keys, values, segment, totals, out_grad = item
    length, width = query.shape
    block = min(512, length)
    scale = width ** (-0.5)
    place = jnp.arange(length)
    query_parts = []
    key_grad = jnp.zeros((length, width), jnp.float32)
    value_grad = jnp.zeros((length, width), jnp.float32)
    for first in range(0, length, block):
        part_query = query[first : first + block]
        part_out = out_grad[first : first + block]
        allowed = (segment[first : first + block, None] == segment[None, :]) & (
            place[first : first + block, None] >= place[None, :]
        )
        scores = jnp.where(allowed, against(part_query, keys) * scale, -1e30)
        probs = jnp.exp(scores - totals[first : first + block, None])
        prob_grad = against(part_out, values)
        inner = jnp.sum(probs * prob_grad, axis=1, keepdims=True)
        score_grad = (probs * (prob_grad - inner) * scale).astype(jnp.bfloat16)
        query_parts.append(product(score_grad, keys))
        key_grad = key_grad + outer(score_grad, part_query)
        value_grad = value_grad + outer(probs.astype(jnp.bfloat16), part_out)
    return (jnp.concatenate(query_parts, axis=0), key_grad, value_grad)


def on_device(
    block_input,
    output_grad,
    document_ids,
    mixer_gain,
    mamba_gate,
    mamba_input,
    mamba_step,
    query_weight,
    key_weight,
    value_weight,
    state_weight,
    input_filter,
    input_shift,
    state_filter,
    state_shift,
    step_bias,
    decay_log,
    skip_gain,
    mixer_out,
    feed_gain,
    feed_gate,
    feed_up,
    feed_down,
):
    sequences, length = document_ids.shape
    rows = block_input.shape[0]
    tokens = sequences * length
    col_count = lax.axis_size("col")
    group_index = lax.axis_index("row") * col_count + lax.axis_index("col")
    pair_head = group_index // (QH // KVH)
    mixer_scale = mixer_gain.astype(jnp.float32)
    feed_scale = feed_gain.astype(jnp.float32)
    residual = block_input.astype(jnp.float32)
    normed_one, inverse_one = norm_forward(residual, mixer_scale)
    tokens_one = row_tokens(normed_one)
    gate_values, input_values, step_values, query_pre = (
        lax.psum_scatter(
            product(tokens_one, mamba_gate).astype(jnp.bfloat16),
            "col",
            scatter_dimension=1,
            tiled=True,
        ).astype(jnp.float32),
        lax.psum_scatter(
            product(tokens_one, mamba_input).astype(jnp.bfloat16),
            "col",
            scatter_dimension=1,
            tiled=True,
        ).astype(jnp.float32),
        lax.psum_scatter(
            product(tokens_one, mamba_step).astype(jnp.bfloat16),
            "col",
            scatter_dimension=1,
            tiled=True,
        ).astype(jnp.float32),
        lax.psum_scatter(
            product(tokens_one, query_weight).astype(jnp.bfloat16),
            "col",
            scatter_dimension=1,
            tiled=True,
        ).astype(jnp.float32),
    )
    pair_weight = jnp.concatenate(
        [
            lax.dynamic_slice_in_dim(key_weight, pair_head * HD, HD, 1),
            lax.dynamic_slice_in_dim(value_weight, pair_head * HD, HD, 1),
        ],
        axis=1,
    )
    state_raw, pair_raw = (
        lax.psum(product(tokens_one, state_weight).astype(jnp.bfloat16), "col").astype(jnp.float32),
        lax.psum(product(tokens_one, pair_weight).astype(jnp.bfloat16), "col").astype(jnp.float32),
    )
    state_conv, state_pull = jax.vjp(
        partial(state_piece, sequences),
        state_raw,
        state_filter.astype(jnp.float32),
        state_shift.astype(jnp.float32),
    )
    gated, mamba_pull = jax.vjp(
        partial(mamba_piece, document_ids),
        input_values,
        gate_values,
        step_values,
        state_conv,
        input_filter.astype(jnp.float32),
        input_shift.astype(jnp.float32),
        step_bias.astype(jnp.float32),
        decay_log.astype(jnp.float32),
        skip_gain.astype(jnp.float32),
    )
    query_low = (
        rotate(query_pre.reshape(sequences, length, 1, HD), 1.0)
        .reshape(sequences, length, HD)
        .astype(jnp.bfloat16)
    )
    key_low = (
        rotate(pair_raw[:, :HD].reshape(sequences, length, 1, HD), 1.0)
        .reshape(sequences, length, HD)
        .astype(jnp.bfloat16)
    )
    value_low = pair_raw[:, HD:].reshape(sequences, length, HD).astype(jnp.bfloat16)
    attended, totals = lax.map(attend_forward, (query_low, key_low, value_low, document_ids))
    features = jnp.concatenate(
        [gated.astype(jnp.bfloat16), attended.reshape(tokens, HD).astype(jnp.bfloat16)], axis=1
    )
    features_row = col_features(features)

    def mixer_term(start, count):
        return product(take_rows(features_row, start, count), mixer_out)

    after_mixer = residual + row_out(mixer_term, rows)
    normed_two, inverse_two = norm_forward(after_mixer, feed_scale)
    tokens_two = row_tokens(normed_two)
    gate, upper = (
        lax.psum_scatter(
            product(tokens_two, feed_gate).astype(jnp.bfloat16),
            "col",
            scatter_dimension=1,
            tiled=True,
        ).astype(jnp.float32),
        lax.psum_scatter(
            product(tokens_two, feed_up).astype(jnp.bfloat16),
            "col",
            scatter_dimension=1,
            tiled=True,
        ).astype(jnp.float32),
    )
    hidden = (jax.nn.silu(gate) * upper).astype(jnp.bfloat16)
    hidden_row = col_features(hidden)

    def feed_term(start, count):
        return product(take_rows(hidden_row, start, count), feed_down)

    block_output = after_mixer + row_out(feed_term, rows)
    grad_tokens = row_tokens(output_grad)
    hidden_grad = rounded(feature_grads(against(grad_tokens, feed_down)))
    sigma = jax.nn.sigmoid(gate)
    gate_grad = (hidden_grad * upper * sigma * (1.0 + gate * (1.0 - sigma))).astype(jnp.bfloat16)
    upper_grad = (hidden_grad * gate * sigma).astype(jnp.bfloat16)
    down_wgrad = outer(hidden_row, grad_tokens)
    gate_row, upper_row = (
        lax.all_gather(gate_grad, "col", axis=1, tiled=True),
        lax.all_gather(upper_grad, "col", axis=1, tiled=True),
    )
    gate_wgrad = outer(tokens_two, gate_row)
    upper_wgrad = outer(tokens_two, upper_row)

    def feed_back(start, count):
        return against(take_rows(gate_row, start, count), feed_gate) + against(
            take_rows(upper_row, start, count), feed_up
        )

    mixed_grad, feed_gain_grad = norm_backward(
        after_mixer, inverse_two, feed_scale, row_out(feed_back, rows)
    )
    mixer_grad = output_grad.astype(jnp.float32) + mixed_grad
    mixer_tokens = row_tokens(mixer_grad.astype(jnp.bfloat16))
    feature_grad = rounded(feature_grads(against(mixer_tokens, mixer_out)))
    out_wgrad = outer(features_row, mixer_tokens)
    span = gated.shape[1]
    attended_grad = feature_grad[:, span:].astype(jnp.bfloat16).reshape(sequences, length, HD)
    query_grad, key_grad, value_grad = lax.map(
        attend_backward, (query_low, key_low, value_low, document_ids, totals, attended_grad)
    )
    query_back = (
        rotate(query_grad.reshape(sequences, length, 1, HD), -1.0)
        .reshape(tokens, HD)
        .astype(jnp.bfloat16)
    )
    key_back = rotate(key_grad.reshape(sequences, length, 1, HD), -1.0).reshape(tokens, HD)
    (
        input_back,
        gate_back,
        step_back,
        state_back,
        filter_wgrad,
        shift_wgrad,
        bias_wgrad,
        decay_wgrad,
        skip_wgrad,
    ) = mamba_pull(feature_grad[:, :span])
    gate_cols, input_cols, step_cols, query_cols = (
        lax.all_gather(gate_back.astype(jnp.bfloat16), "col", axis=1, tiled=True),
        lax.all_gather(input_back.astype(jnp.bfloat16), "col", axis=1, tiled=True),
        lax.all_gather(step_back.astype(jnp.bfloat16), "col", axis=1, tiled=True),
        lax.all_gather(query_back, "col", axis=1, tiled=True),
    )
    state_cols, pair_cols = (
        lax.all_gather(state_back.astype(jnp.bfloat16), "col", axis=1, tiled=True).astype(
            state_back.dtype
        ),
        lax.all_gather(
            as_sent(jnp.concatenate([key_back, value_grad.reshape(tokens, HD)], axis=1)),
            "col",
            axis=1,
            tiled=True,
        ),
    )
    state_sum = jnp.sum(state_cols.reshape(tokens, col_count, -1), axis=1)
    pair_sum = jnp.sum(pair_cols.reshape(tokens, col_count, -1), axis=1)
    state_raw_grad, state_filter_grad, state_shift_grad = state_pull(state_sum)
    tokens_exact = tokens_one.astype(jnp.float32)
    state_wgrad = exact_outer(tokens_exact, state_raw_grad)
    pair_wgrad = exact_outer(tokens_exact, pair_sum)
    key_wgrad = lax.dynamic_update_slice_in_dim(
        jnp.zeros(key_weight.shape, jnp.float32), pair_wgrad[:, :HD], pair_head * HD, 1
    )
    value_wgrad = lax.dynamic_update_slice_in_dim(
        jnp.zeros(value_weight.shape, jnp.float32), pair_wgrad[:, HD:], pair_head * HD, 1
    )
    gate_proj_wgrad = outer(tokens_one, gate_cols)
    input_proj_wgrad = outer(tokens_one, input_cols)
    step_proj_wgrad = outer(tokens_one, step_cols)
    query_wgrad = outer(tokens_one, query_cols)
    state_exact = state_weight.astype(jnp.float32)
    pair_exact = pair_weight.astype(jnp.float32)

    def mixer_back(start, count):
        total = against(take_rows(gate_cols, start, count), mamba_gate) + against(
            take_rows(input_cols, start, count), mamba_input
        )
        total = (
            total
            + against(take_rows(step_cols, start, count), mamba_step)
            + against(take_rows(query_cols, start, count), query_weight)
        )
        total = total + exact_against(take_rows(state_raw_grad, start, count), state_exact)
        return total + exact_against(take_rows(pair_sum, start, count), pair_exact)

    input_norm_grad, mixer_gain_grad = norm_backward(
        residual, inverse_one, mixer_scale, row_out(mixer_back, rows)
    )
    input_grad = mixer_grad + input_norm_grad
    shared = lax.psum(
        (
            mixer_gain_grad,
            key_wgrad,
            value_wgrad,
            state_wgrad,
            state_filter_grad,
            state_shift_grad,
            feed_gain_grad,
        ),
        ("dp", "row"),
    )
    mixer_sums = (
        lax.psum(gate_proj_wgrad.astype(jnp.bfloat16), "dp").astype(jnp.float32),
        lax.psum(input_proj_wgrad.astype(jnp.bfloat16), "dp").astype(jnp.float32),
        lax.psum(step_proj_wgrad.astype(jnp.bfloat16), "dp").astype(jnp.float32),
        lax.psum(query_wgrad.astype(jnp.bfloat16), "dp").astype(jnp.float32),
        lax.psum(filter_wgrad.astype(jnp.bfloat16), "dp").astype(jnp.float32),
        lax.psum(shift_wgrad.astype(jnp.bfloat16), "dp").astype(jnp.float32),
        lax.psum(bias_wgrad.astype(jnp.bfloat16), "dp").astype(jnp.float32),
        lax.psum(decay_wgrad.astype(jnp.bfloat16), "dp").astype(jnp.float32),
        lax.psum(skip_wgrad.astype(jnp.bfloat16), "dp").astype(jnp.float32),
        lax.psum(out_wgrad.astype(jnp.bfloat16), "dp").astype(jnp.float32),
    )
    feed_sums = feed_sum(gate_wgrad, upper_wgrad, down_wgrad)
    return (
        block_output,
        input_grad,
        shared[0],
        mixer_sums[0],
        mixer_sums[1],
        mixer_sums[2],
        mixer_sums[3],
        shared[1],
        shared[2],
        shared[3],
        mixer_sums[4],
        mixer_sums[5],
        shared[4],
        shared[5],
        mixer_sums[6],
        mixer_sums[7],
        mixer_sums[8],
        mixer_sums[9],
        shared[6],
        feed_sums[0],
        feed_sums[1],
        feed_sums[2],
    )


def solution(mesh):
    placed = (
        P(("dp", "row"), "col"),
        P(("dp", "row"), "col"),
        P("dp", None),
        P("col"),
        P("col", "row"),
        P("col", "row"),
        P("col", "row"),
        P("col", "row"),
        P("col", None),
        P("col", None),
        P("col", None),
        P(("row", "col"), None),
        P(("row", "col")),
        P(),
        P(),
        P(("row", "col")),
        P(("row", "col")),
        P(("row", "col")),
        P("row", "col"),
        P("col"),
        P("col", "row"),
        P("col", "row"),
        P("row", "col"),
    )
    return jax.shard_map(
        on_device,
        mesh=mesh,
        in_specs=placed,
        out_specs=(
            P(("dp", "row"), "col"),
            P(("dp", "row"), "col"),
            P("col"),
            P("col", "row"),
            P("col", "row"),
            P("col", "row"),
            P("col", "row"),
            P("col", None),
            P("col", None),
            P("col", None),
            P(("row", "col"), None),
            P(("row", "col")),
            P(),
            P(),
            P(("row", "col")),
            P(("row", "col")),
            P(("row", "col")),
            P("row", "col"),
            P("col"),
            P("col", "row"),
            P("col", "row"),
            P("row", "col"),
        ),
        check_vma=False,
    )
```

profile of v0, /device:TPU:0, one launch (start us, length us, event | category | flops | bytes accessed | tf_op | source)
XLA Modules:
  0.0 923.2 jit_solution(10999309485020936223)
XLA Ops:
  8.4 2.6 psum.182
  15.3 28.1 %all-gather.14.cloned.1.call-done = bf16[1024,512]{1,0:T(8,128)(2,1)} async-done(((bf16[256,512]{1,0:T(8,128)(2,1)}), bf16[1024,512]{1,0:T(8,128)(2,1)}) %all-gather.14.cloned.1.call-update) | async-done | bytes 1048592 | tf_op jit(solution)/shard_map/all_gather | solution.py:69
  43.4 2.5 convolution_convert_fusion.16
  56.4 3.4 all-reduce.22
  64.0 14.0 %all-reduce.36.cloned.1.call-done = (bf16[1024,128]{0,1:T(8,128)(2,1)}, bf16[1024,256]{1,0:T(8,128)(2,1)}) async-done(((bf16[1024,128]{0,1:T(8,128)(2,1)}, bf16[1024,256]{1,0:T(8,128)(2,1)}), (bf16[1024,128]{0,1:T(8,128)(2,1)}, bf16[1024,256]{1,0:T(8,128)(2,1)})) %all-reduce.36.cloned.1.call-update) | async-done | bytes 786448 | tf_op jit(solution)/shard_map/psum | solution.py:344
  92.2 2.8 fusion.142
  97.6 67.1 %while.57 = (s32[]{:T(128)}, f32[1,3,128,64]{2,3,1,0:T(8,128)S(1)}, s32[1]{0:T(128)}, f32[4,1,256,3,64]{2,0,4,3,1:T(4,128)S(1)}, f32[4,1,3,128,64]{3,4,2,1,0:T(8...) while((s32[]{:T(128)}, f32[1,3,128,64]{2,3,1,0:T(8,128)S(1)}, ...), condition=%wide.region_8.9_spmd.clone, body=%wide.region_5.0_spmd.clone.sunk | while | flops 404157952 | bytes 3645057 | solution.py:176
  110.8 2.8 dynamic_update_slice.98
  127.6 2.8 dynamic_update_slice.98
  144.3 2.8 dynamic_update_slice.98
  161.1 2.8 dynamic_update_slice.98
  169.3 10.3 %all-gather.16.cloned.1.call-done = bf16[1024,512]{0,1:T(8,128)(2,1)} async-done(((bf16[1024,256]{0,1:T(8,128)(2,1)}), bf16[1024,512]{0,1:T(8,128)(2,1)}) %all-gather.16.cloned.1.call-update) | async-done | bytes 1048592 | tf_op jit(solution)/shard_map/all_gather | solution.py:73
  179.6 3.1 convolution_convert_fusion.5
  183.5 28.5 %reduce-scatter.18.cloned.1.call-done = bf16[256,512]{1,0:T(8,128)(2,1)} async-done(((bf16[1024,512]{1,0:T(8,128)(2,1)}), bf16[256,512]{1,0:T(8,128)(2,1)}) %reduce-scatter.18.cloned.1.call-update) | async-done | bytes 262160 | tf_op jit(solution)/shard_map/reduce_scatter | solution.py:83
  213.1 2.5 psum.185
  217.4 23.2 %all-gather.22.cloned.1.call-done = bf16[1024,512]{1,0:T(8,128)(2,1)} async-done(((bf16[256,512]{1,0:T(8,128)(2,1)}), bf16[1024,512]{1,0:T(8,128)(2,1)}) %all-gather.22.cloned.1.call-update) | async-done | bytes 1048592 | tf_op jit(solution)/shard_map/all_gather | solution.py:69
  240.6 3.1 convolution_convert_fusion.1
  244.0 25.9 %all-gather.18.cloned.1.call-done = bf16[1024,512]{1,0:T(8,128)(2,1)} async-done(((bf16[256,512]{1,0:T(8,128)(2,1)}), bf16[1024,512]{1,0:T(8,128)(2,1)}) %all-gather.18.cloned.1.call-update) | async-done | bytes 1048592 | tf_op jit(solution)/shard_map/all_gather | solution.py:69
  269.9 3.0 convolution_convert_fusion.3
  273.0 2.9 convolution_convert_fusion.4
  276.0 5.2 reduce-scatter.26.cloned.1.call-done
  281.2 12.6 %reduce-scatter.22.cloned.1.call-done = bf16[1024,256]{1,0:T(8,128)(2,1)} async-done(((bf16[1024,512]{1,0:T(8,128)(2,1)}), bf16[1024,256]{1,0:T(8,128)(2,1)}) %reduce-scatter.22.cloned.1.call-update) | async-done | bytes 524304 | tf_op jit(solution)/shard_map/reduce_scatter | solution.py:394
  293.7 12.5 %reduce-scatter.20.cloned.1.call-done = bf16[1024,256]{1,0:T(8,128)(2,1)} async-done(((bf16[1024,512]{1,0:T(8,128)(2,1)}), bf16[1024,256]{1,0:T(8,128)(2,1)}) %reduce-scatter.20.cloned.1.call-update) | async-done | bytes 524304 | tf_op jit(solution)/shard_map/reduce_scatter | solution.py:388
  306.2 3.2 fusion.121
  310.0 9.7 %all-gather.24.cloned.1.call-done = bf16[1024,512]{1,0:T(8,128)(2,1)} async-done(((bf16[1024,256]{1,0:T(8,128)(2,1)}), bf16[1024,512]{1,0:T(8,128)(2,1)}) %all-gather.24.cloned.1.call-update) | async-done | bytes 1048592 | tf_op jit(solution)/shard_map/all_gather | solution.py:415
  319.7 3.3 fusion.242
  323.1 8.9 all-gather.26.cloned.1.call-done
  331.9 3.8 add_convert_fusion.1
  335.8 29.0 %reduce-scatter.28.cloned.1.call-done = bf16[256,512]{1,0:T(8,128)(2,1)} async-done(((bf16[1024,512]{1,0:T(8,128)(2,1)}), bf16[256,512]{1,0:T(8,128)(2,1)}) %reduce-scatter.28.cloned.1.call-update) | async-done | bytes 262160 | tf_op jit(solution)/shard_map/reduce_scatter | solution.py:83
  366.6 2.4 psum.186
  371.6 26.1 %all-gather.28.cloned.1.call-done = bf16[1024,512]{1,0:T(8,128)(2,1)} async-done(((bf16[256,512]{1,0:T(8,128)(2,1)}), bf16[1024,512]{1,0:T(8,128)(2,1)}) %all-gather.28.cloned.1.call-update) | async-done | bytes 1048592 | tf_op jit(solution)/shard_map/all_gather | solution.py:69
  397.7 3.1 convolution_convert_fusion
  401.0 3.2 convolution_convert_fusion.11
  405.7 3.0 all-gather.20.cloned.1.call-done
  408.8 3.2 convolution_convert_fusion.9
  413.5 7.8 reduce-scatter.30.cloned.1.call-done
  428.9 2.4 multiply_reduce_fusion.4
  434.5 2.9 all_gather.50
  437.4 2.4 reshape.1475
  443.0 142.4 %while.58 = (s32[]{:T(128)}, f32[3]{0:T(128)}, f32[1,3,128,64]{2,3,1,0:T(8,128)}, f32[4,1,256,3,64]{2,0,4,3,1:T(4,128)}, f32[4,1,256,3]{2,3,1,0:T(4,128)}, /*ind...) while((s32[]{:T(128)}, f32[3]{0:T(128)}, ...), condition=%wide.region_40.41_spmd.clone, body=%wide.region_27.40_spmd.clone.sunk | while | flops 986376448 | bytes 10811398 | solution.py:176
  465.1 3.8 reduce-window.74
  472.6 5.3 dynamic_update_slice.103
  500.9 3.8 reduce-window.74
  508.5 5.3 dynamic_update_slice.103
  536.7 3.8 reduce-window.74
  544.3 5.3 dynamic_update_slice.103
  572.6 3.8 reduce-window.74
  580.1 5.3 dynamic_update_slice.103
  589.5 2.8 multiply_convert_fusion
  602.7 2.6 all-gather
  609.5 2.5 all_gather.55
  613.2 2.9 fusion.209
  622.2 3.3 reshape.1493
  625.5 5.1 reduce_sum.342
  630.6 3.5 multiply_reduce_fusion.8
  640.5 3.0 convolution_convert_fusion.2
  646.8 3.4 fusion.245
  650.8 20.2 %all-reduce.25 = (bf16[512,6]{0,1:T(8,128)(2,1)S(1)}, bf16[192,4]{0,1:T(4,128)(2,1)S(1)}, bf16[192]{0:T(256)(128)(2,1)S(1)}, bf16[3]{0:T(256)(128)(2,1)S(1)}, bf...) all-reduce(bf16[512,6]{0,1:T(8,128)(2,1)S(1)} %convolution_convert_, ...), channel_id=1, replica_groups=mesh['dp'=4,'row'=4,'col'=2] {'dp'}, use_global_device_ids=true, to_apply=%region_52.53 | all-reduce | flops 4041 | bytes 16164 | tf_op jit(solution)/shard_map/psum | solution.py:522
  674.2 55.9 %all-reduce.34.cloned.1.call-done = (bf16[512,384]{1,0:T(8,128)(2,1)}, bf16[512,384]{1,0:T(8,128)(2,1)}, bf16[512,128]{1,0:T(8,128)(2,1)}, bf16[512,512]{1,0:T(8...) async-done(((bf16[512,384]{1,0:T(8,128)(2,1)}, bf16[512,384]{1,0:T(8,128)(2,1)}, bf16[512,128]{1,0:T(8,128)(2,1)}, ...) | async-done | bytes 3014672 | tf_op jit(solution)/shard_map/psum | solution.py:520
  740.3 19.3 %reduce-scatter.32.cloned.1.call-done = bf16[256,512]{1,0:T(8,128)(2,1)} async-done(((bf16[1024,512]{1,0:T(8,128)(2,1)}), bf16[256,512]{1,0:T(8,128)(2,1)}) %reduce-scatter.32.cloned.1.call-update) | async-done | bytes 262160 | tf_op jit(solution)/shard_map/reduce_scatter | solution.py:83
  760.8 2.5 psum.187
  763.3 42.7 %all-reduce.23 = (f32[512]{0:T(512)}, f32[256,4]{0,1:T(4,128)}, f32[256]{0:T(256)}, f32[512]{0:T(512)}) all-reduce(f32[512]{0:T(512)S(1)} %get-tuple-element.863, f32[256,4]{0,1:T(4,128)S(1)} %pad_add_fusion.6, f32[256]{0:T(256)S(1)} %get-tuple-element.857, f32[512]{0:T(512)S(1)} %copy-done.112), channel_id=1, replica_groups=mesh['dp'=4,'row'=4,'col'=2] {'dp','row'}, use_global_device_ids=true, to_apply=%region_49.50 | all-reduce | flops 2304 | bytes 18432 | tf_op jit(solution)/shard_map/psum | solution.py:507
  806.1 2.4 fusion.147
  808.5 102.7 %all-reduce.32.cloned.1.call-done = (f32[512,128]{1,0:T(8,128)}, f32[512,128]{1,0:T(8,128)}, f32[512,256]{1,0:T(8,128)}) async-done(((f32[512,128]{1,0:T(8,128)}, f32[512,128]{1,0:T(8,128)}, f32[512,256]{1,0:T(8,128)}), (f32[512,128]{1,0:T(8,128)}, f32[512,128]{1,0:T(8,128)}, f32[512,256]{1,0:T(8,128)})) %all-reduce.32.cloned.1.call-update) | async-done | bytes 1048592 | tf_op jit(solution)/shard_map/psum | solution.py:507
  (866 shorter events, 271.5 us)
Async XLA Ops:
  7.2 265.8 %copy-start = (bf16[512,512]{1,0:T(8,128)(2,1)S(1)}, bf16[512,512]{1,0:T(8,128)(2,1)}, u32[]{:S(2)}) copy-start(bf16[512,512]{1,0:T(8,128)(2,1)} %param.47) | copy-start | bytes 1572868
  7.2 36.2 %all-gather.14.cloned.1.call-start = ((), (), s32[]{:S(2)}) async-start(), calls=%async_computation.11 | async-start | bytes 1310720 | tf_op jit(solution)/shard_map/all_gather | solution.py:69
  14.0 33.3 %copy-start.41 = (bf16[512,256]{1,0:T(8,128)(2,1)S(1)}, bf16[512,256]{1,0:T(8,128)(2,1)}, u32[]{:S(2)}) copy-start(bf16[512,256]{1,0:T(8,128)(2,1)} %param.37) | copy-start | bytes 786436
  14.1 49.0 %reduce-scatter.16.cloned.1.call-start = ((), (), s32[]{:S(2)}) async-start(), calls=%async_computation.14 | async-start | bytes 393216 | tf_op jit(solution)/shard_map/reduce_scatter | solution.py:328
  15.3 33.3 %copy-start.34 = (bf16[512,64]{1,0:T(8,128)(2,1)}, bf16[512,64]{1,0:T(8,128)(2,1)S(1)}, u32[]{:S(2)}) copy-start(bf16[512,64]{1,0:T(8,128)(2,1)S(1)} %get-tuple-element.1024) | copy-start | bytes 196612
  15.3 33.2 %copy-start.36 = (bf16[512,64]{1,0:T(8,128)(2,1)}, bf16[512,64]{1,0:T(8,128)(2,1)S(1)}, u32[]{:S(2)}) copy-start(bf16[512,64]{1,0:T(8,128)(2,1)S(1)} %get-tuple-element.1025) | copy-start | bytes 196612
  46.0 32.1 %all-reduce.36.cloned.1.call-start = ((), (), s32[]{:S(2)}) async-start(), calls=%async_computation.33 | async-start | bytes 1572864 | tf_op jit(solution)/shard_map/psum | solution.py:344
  48.6 41.6 %reduce-scatter.12.cloned.1.call-start = ((), (), s32[]{:S(2)}) async-start(), calls=%async_computation.12 | async-start | bytes 1179648 | tf_op jit(solution)/shard_map/reduce_scatter | solution.py:316
  49.3 12.0 %copy-start.61 = (bf16[512,384]{1,0:T(8,128)(2,1)S(1)}, bf16[512,384]{1,0:T(8,128)(2,1)}, u32[]{:S(2)}) copy-start(bf16[512,384]{1,0:T(8,128)(2,1)} %param.31) | copy-start | bytes 1179652
  50.8 116.0 %reduce-scatter.14.cloned.1.call-start = ((), (), s32[]{:S(2)}) async-start(), calls=%async_computation.13 | async-start | bytes 1179648 | tf_op jit(solution)/shard_map/reduce_scatter | solution.py:310
  50.9 29.2 %copy-start.132 = (f32[32]{0:T(128)}, f32[32]{0:T(128)S(1)}, u32[]{:S(2)}) copy-start(f32[32]{0:T(128)S(1)} %multiply_power_fusion) | copy-start | bytes 388
  51.0 11.8 %copy-start.128 = (f32[3]{0:T(128)}, f32[3]{0:T(128)S(1)}, u32[]{:S(2)}) copy-start(f32[3]{0:T(128)S(1)} %convert_element_type.435) | copy-start | bytes 40
  52.3 380.2 %copy-start.85 = (f32[192]{0:T(256)}, f32[192]{0:T(256)S(1)}, u32[]{:S(2)}) copy-start(f32[192]{0:T(256)S(1)} %mul.1220) | copy-start | bytes 2308
  54.1 26.0 %copy-start.73 = (f32[1024]{0:T(1024)}, f32[1024]{0:T(1024)S(1)}, u32[]{:S(2)}) copy-start(f32[1024]{0:T(1024)S(1)} %iota_convert_fusion) | copy-start | bytes 12292
  54.2 37.1 %copy-start.92 = (f32[192,1]{0,1:T(1,128)}, f32[192,1]{0,1:T(1,128)S(1)}, u32[]{:S(2)}) copy-start(f32[192,1]{0,1:T(1,128)S(1)} %get-tuple-element.1010) | copy-start | bytes 2308
  54.2 37.1 %copy-start.94 = (f32[192,1]{0,1:T(1,128)}, f32[192,1]{0,1:T(1,128)S(1)}, u32[]{:S(2)}) copy-start(f32[192,1]{0,1:T(1,128)S(1)} %get-tuple-element.1011) | copy-start | bytes 2308
  54.2 37.1 %copy-start.96 = (f32[192,1]{0,1:T(1,128)}, f32[192,1]{0,1:T(1,128)S(1)}, u32[]{:S(2)}) copy-start(f32[192,1]{0,1:T(1,128)S(1)} %get-tuple-element.1012) | copy-start | bytes 2308
  54.2 37.1 %copy-start.98 = (f32[192,1]{0,1:T(1,128)}, f32[192,1]{0,1:T(1,128)S(1)}, u32[]{:S(2)}) copy-start(f32[192,1]{0,1:T(1,128)S(1)} %get-tuple-element.1013) | copy-start | bytes 2308
  54.8 32.7 %copy-start.100 = (f32[256,1]{0,1:T(1,128)}, f32[256,1]{0,1:T(1,128)S(1)}, u32[]{:S(2)}) copy-start(f32[256,1]{0,1:T(1,128)S(1)} %get-tuple-element.1006) | copy-start | bytes 3076
  54.8 32.7 %copy-start.102 = (f32[256,1]{0,1:T(1,128)}, f32[256,1]{0,1:T(1,128)S(1)}, u32[]{:S(2)}) copy-start(f32[256,1]{0,1:T(1,128)S(1)} %get-tuple-element.1007) | copy-start | bytes 3076
  54.8 32.7 %copy-start.104 = (f32[256,1]{0,1:T(1,128)}, f32[256,1]{0,1:T(1,128)S(1)}, u32[]{:S(2)}) copy-start(f32[256,1]{0,1:T(1,128)S(1)} %get-tuple-element.1008) | copy-start | bytes 3076
  59.8 18.2 %copy-start.70 = (bf16[1024,6]{0,1:T(8,128)(2,1)}, bf16[1024,6]{0,1:T(8,128)(2,1)S(1)}, u32[]{:S(2)}) copy-start(bf16[1024,6]{0,1:T(8,128)(2,1)S(1)} %all-reduce.22) | copy-start | bytes 36868
  62.8 116.8 %all-gather.16.cloned.1.call-start = ((), (), s32[]{:S(2)}) async-start(), calls=%async_computation.15 | async-start | bytes 1572864 | tf_op jit(solution)/shard_map/all_gather | solution.py:73
  169.2 14.3 %copy-start.136 = (bf16[512]{0:T(512)(128)(2,1)S(1)}, bf16[512]{0:T(512)(128)(2,1)}, u32[]{:S(2)}) copy-start(bf16[512]{0:T(512)(128)(2,1)} %param.46) | copy-start | bytes 3076
  169.2 42.8 %copy-start.7 = (bf16[256,512]{1,0:T(8,128)(2,1)S(1)}, bf16[256,512]{1,0:T(8,128)(2,1)}, u32[]{:S(2)}) copy-start(bf16[256,512]{1,0:T(8,128)(2,1)} %param.27) | copy-start | bytes 786436
  169.2 42.8 %reduce-scatter.18.cloned.1.call-start = ((), (), s32[]{:S(2)}) async-start(), calls=%async_computation.16 | async-start | bytes 1310720 | tf_op jit(solution)/shard_map/reduce_scatter | solution.py:83
  182.7 57.9 %all-gather.22.cloned.1.call-start = ((), (), s32[]{:S(2)}) async-start(), calls=%async_computation.22 | async-start | bytes 1310720 | tf_op jit(solution)/shard_map/all_gather | solution.py:69
  183.4 86.4 %all-gather.18.cloned.1.call-start = ((), (), s32[]{:S(2)}) async-start(), calls=%async_computation.17 | async-start | bytes 1310720 | tf_op jit(solution)/shard_map/all_gather | solution.py:69
  183.5 185.6 %copy-start.71 = (f32[512]{0:T(512)}, f32[512]{0:T(512)S(1)}, u32[]{:S(2)}) copy-start(f32[512]{0:T(512)S(1)} %convert_element_type.458) | copy-start | bytes 6148
  215.6 153.5 %copy-start.81 = (f32[256]{0:T(256)}, f32[256]{0:T(256)S(1)}, u32[]{:S(2)}) copy-start(f32[256]{0:T(256)S(1)} %add_rsqrt_fusion) | copy-start | bytes 3076
  217.4 63.8 %reduce-scatter.26.cloned.1.call-start = ((), (), s32[]{:S(2)}) async-start(), calls=%async_computation.23 | async-start | bytes 1572864 | tf_op jit(solution)/shard_map/reduce_scatter | solution.py:77
  243.7 50.0 %reduce-scatter.22.cloned.1.call-start = ((), (), s32[]{:S(2)}) async-start(), calls=%async_computation.19 | async-start | bytes 1572864 | tf_op jit(solution)/shard_map/reduce_scatter | solution.py:394
  272.9 33.3 %reduce-scatter.20.cloned.1.call-start = ((), (), s32[]{:S(2)}) async-start(), calls=%async_computation.18 | async-start | bytes 1572864 | tf_op jit(solution)/shard_map/reduce_scatter | solution.py:388
  275.9 43.8 %all-gather.24.cloned.1.call-start = ((), (), s32[]{:S(2)}) async-start(), calls=%async_computation.24 | async-start | bytes 1572864 | tf_op jit(solution)/shard_map/all_gather | solution.py:415
  309.4 22.5 %all-gather.26.cloned.1.call-start = ((), (), s32[]{:S(2)}) async-start(), calls=%async_computation.25 | async-start | bytes 1572864 | tf_op jit(solution)/shard_map/all_gather | solution.py:416
  310.0 54.8 %reduce-scatter.28.cloned.1.call-start = ((), (), s32[]{:S(2)}) async-start(), calls=%async_computation.26 | async-start | bytes 1310720 | tf_op jit(solution)/shard_map/reduce_scatter | solution.py:83
  323.1 41.8 %copy-start.16 = (bf16[256,512]{1,0:T(8,128)(2,1)S(1)}, bf16[256,512]{1,0:T(8,128)(2,1)}, u32[]{:S(2)}) copy-start(bf16[256,512]{1,0:T(8,128)(2,1)} %reduce-scatter.18.cloned.1.call-done) | copy-start | bytes 786436
  323.1 46.0 %copy-start.27 = (bf16[256,512]{1,0:T(8,128)(2,1)S(1)}, bf16[256,512]{1,0:T(8,128)(2,1)}, u32[]{:S(2)}) copy-start(bf16[256,512]{1,0:T(8,128)(2,1)} %param.28) | copy-start | bytes 786436
  335.7 62.0 %all-gather.28.cloned.1.call-start = ((), (), s32[]{:S(2)}) async-start(), calls=%async_computation.27 | async-start | bytes 1310720 | tf_op jit(solution)/shard_map/all_gather | solution.py:69
  369.1 31.7 %copy-start.90 = (f32[256]{0:T(256)}, f32[256]{0:T(256)S(1)}, u32[]{:S(2)}) copy-start(f32[256]{0:T(256)S(1)} %fusion.214) | copy-start | bytes 3076
  371.0 37.8 %all-gather.20.cloned.1.call-start = ((), (), s32[]{:S(2)}) async-start(), calls=%async_computation.20 | async-start | bytes 1572864 | tf_op jit(solution)/shard_map/all_gather | solution.py:73
  371.6 29.4 %copy-start.116 = (f32[512]{0:T(512)S(1)}, f32[512]{0:T(512)}, u32[]{:S(2)}) copy-start(f32[512]{0:T(512)} %copy-done.115) | copy-start | bytes 6148
  371.6 29.3 %copy-start.118 = (f32[512]{0:T(512)S(1)}, f32[512]{0:T(512)}, u32[]{:S(2)}) copy-start(f32[512]{0:T(512)} %copy-done.117) | copy-start | bytes 6148
  371.6 29.4 %copy-start.120 = (f32[512]{0:T(512)S(1)}, f32[512]{0:T(512)}, u32[]{:S(2)}) copy-start(f32[512]{0:T(512)} %copy-done.119) | copy-start | bytes 6148
  371.6 29.4 %copy-start.122 = (f32[512]{0:T(512)S(1)}, f32[512]{0:T(512)}, u32[]{:S(2)}) copy-start(f32[512]{0:T(512)} %copy-done.121) | copy-start | bytes 6148
  371.6 49.7 %reduce-scatter.30.cloned.1.call-start = ((), (), s32[]{:S(2)}) async-start(), calls=%async_computation.28 | async-start | bytes 1572864 | tf_op jit(solution)/shard_map/reduce_scatter | solution.py:77
  400.8 221.3 %all-gather.30.cloned.1.call-start = ((), (), s32[]{:S(2)}) async-start(), calls=%async_computation.30 | async-start | bytes 1572864 | tf_op jit(solution)/shard_map/all_gather | solution.py:462
  401.0 30.3 %copy-start.75 = (f32[512]{0:T(512)}, f32[512]{0:T(512)S(1)}, u32[]{:S(2)}) copy-start(f32[512]{0:T(512)S(1)} %log_add_fusion) | copy-start | bytes 6148
  412.0 11.5 %copy-start.44 = (bf16[1024,128]{0,1:T(8,128)(2,1)S(1)}, bf16[1024,128]{0,1:T(8,128)(2,1)}, u32[]{:S(2)}) copy-start(bf16[1024,128]{0,1:T(8,128)(2,1)} %get-tuple-element.941) | copy-start | bytes 786436
  589.0 141.1 %all-reduce.34.cloned.1.call-start = ((), (), s32[]{:S(2)}) async-start(), calls=%async_computation.32 | async-start | bytes 6029312 | tf_op jit(solution)/shard_map/psum | solution.py:520
  609.4 150.2 %reduce-scatter.32.cloned.1.call-start = ((), (), s32[]{:S(2)}) async-start(), calls=%async_computation.29 | async-start | bytes 1310720 | tf_op jit(solution)/shard_map/reduce_scatter | solution.py:83
  640.5 165.6 %reduce-scatter.24.cloned.1.call-start = ((), (), s32[]{:S(2)}) async-start(), calls=%async_computation.21 | async-start | bytes 1310720 | tf_op jit(solution)/shard_map/reduce_scatter | solution.py:83
  643.6 267.6 %all-reduce.32.cloned.1.call-start = ((), (), s32[]{:S(2)}) async-start(), calls=%async_computation.31 | async-start | bytes 2097152 | tf_op jit(solution)/shard_map/psum | solution.py:507
  736.9 22.7 %copy-start.80 = (f32[512]{0:T(512)S(1)}, f32[512]{0:T(512)}, u32[]{:S(2)}) copy-start(f32[512]{0:T(512)} %copy-done.79) | copy-start | bytes 6148
  736.9 22.7 %copy-start.84 = (f32[256]{0:T(256)S(1)}, f32[256]{0:T(256)}, u32[]{:S(2)}) copy-start(f32[256]{0:T(256)} %copy-done.83) | copy-start | bytes 3076
  738.0 25.3 %copy-start.112 = (f32[512]{0:T(512)S(1)}, f32[512]{0:T(512)}, u32[]{:S(2)}) copy-start(f32[512]{0:T(512)} %get-tuple-element.859) | copy-start | bytes 6148
  738.0 68.0 %copy-start.109 = (f32[256]{0:T(256)S(1)}, f32[256]{0:T(256)}, u32[]{:S(2)}) copy-start(f32[256]{0:T(256)} %copy-done.108) | copy-start | bytes 3076
  738.0 68.0 %copy-start.17 = (bf16[256,512]{1,0:T(8,128)(2,1)S(1)}, bf16[256,512]{1,0:T(8,128)(2,1)}, u32[]{:S(2)}) copy-start(bf16[256,512]{1,0:T(8,128)(2,1)} %reduce-scatter.18.cloned.1.call-done) | copy-start | bytes 786436
  738.0 68.0 %copy-start.26 = (bf16[256,512]{1,0:T(8,128)(2,1)S(1)}, bf16[256,512]{1,0:T(8,128)(2,1)}, u32[]{:S(2)}) copy-start(bf16[256,512]{1,0:T(8,128)(2,1)} %reduce-scatter.28.cloned.1.call-done) | copy-start | bytes 786436
  738.0 68.0 %copy-start.28 = (bf16[256,512]{1,0:T(8,128)(2,1)S(1)}, bf16[256,512]{1,0:T(8,128)(2,1)}, u32[]{:S(2)}) copy-start(bf16[256,512]{1,0:T(8,128)(2,1)} %param.28) | copy-start | bytes 786436
  738.0 68.0 %copy-start.72 = (f32[512]{0:T(512)S(1)}, f32[512]{0:T(512)}, u32[]{:S(2)}) copy-start(f32[512]{0:T(512)} %copy-done.71) | copy-start | bytes 6148
  738.0 68.0 %copy-start.82 = (f32[256]{0:T(256)S(1)}, f32[256]{0:T(256)}, u32[]{:S(2)}) copy-start(f32[256]{0:T(256)} %copy-done.81) | copy-start | bytes 3076
  738.1 68.0 %copy-start.91 = (f32[256]{0:T(256)S(1)}, f32[256]{0:T(256)}, u32[]{:S(2)}) copy-start(f32[256]{0:T(256)} %copy-done.90) | copy-start | bytes 3076
  806.0 110.4 %copy-start.1 = (bf16[512,512]{1,0:T(8,128)(2,1)S(1)}, bf16[512,512]{1,0:T(8,128)(2,1)}, u32[]{:S(2)}) copy-start(bf16[512,512]{1,0:T(8,128)(2,1)} %param.47) | copy-start | bytes 1572868
  (126 other events, 457.0 us)
Sparse Core Ops, SparseCore 0:
  14.2 29.1 all-gather.13
  46.2 7.6 reduce-scatter.15
  57.6 20.3 all-reduce.35
  80.7 9.4 reduce-scatter.11
  92.9 9.3 reduce-scatter.13
  169.3 10.2 all-gather.15
  183.1 28.8 reduce-scatter.17
  214.0 26.6 all-gather.21
  243.2 26.6 all-gather.17
  272.6 8.5 reduce-scatter.25
  284.0 9.6 reduce-scatter.21
  296.5 9.6 reduce-scatter.19
  309.5 10.1 all-gather.23
  321.7 10.1 all-gather.25
  335.9 28.9 reduce-scatter.27
  371.1 26.6 all-gather.27
  399.8 8.9 all-gather.19
  411.6 9.7 reduce-scatter.29
  589.2 10.1 all-gather.29
  609.5 120.5 all-reduce.33
  733.1 26.5 reduce-scatter.31
  762.8 28.6 reduce-scatter.23
  798.2 112.9 all-reduce.31
where the time goes:
time: 930 us; the launch traced here: 923 us
  waiting for transfers between devices  425 us (46%)
  matrix products  137 us (15%)
  other arithmetic  123 us (13%)
  local copies, waits for them, and re-layouts  120 us (13%)
  blocking collectives  88.1 us (9%)
  between operations  16.8 us (2%)
  loops' own time  11.8 us (1%)
    all_gather x4, waiting for transfers between devices, row_tokens(): return lax.all_gather(values, 'row', axis=0, tiled=True)  103 us
    psum x1, waiting for transfers between devices, on_device(): lax.psum((mixer_gain_grad, key_wgrad, value_wgrad, state_wgrad, state_fil...  103 us
    reduce_scatter x4, waiting for transfers between devices, row_out(): lax.psum_scatter(term(jnp.int32(0), lax.axis_size('row') * rows).astype(j...  76.9 us
    psum x1, waiting for transfers between devices, on_device(): lax.psum(gate_proj_wgrad.astype(jnp.bfloat16), 'dp').astype(jnp.float32)  55.9 us
    psum x1, blocking collectives, on_device(): lax.psum((mixer_gain_grad, key_wgrad, value_wgrad, state_wgrad, state_fil...  42.7 us
    dynamic_update_slice x28, local copies, waits for them, and re-layouts, ssd_scan(): lax.scan(jax.checkpoint(advance), start, (split(inputs), split(steps), sp...  42.3 us
    another operation x44, other arithmetic  31.2 us
    dot_general x12, matrix products, against(): lax.dot_general(left, right, (((1,), (1,)), ((), ())), preferred_element_...  28.9 us
  transfers between devices with their start and end apart: 23, of which 18 were waited for; matrix products, arithmetic and copies ran while one was open for 20% of the time, Pallas kernels for 0%

commit v1 on v0

v1 whole, which is shorter than its diff:
```python
import jax
import jax.numpy as jnp
from jax import lax
from jax.experimental import pallas as pl
from jax.experimental.pallas import tpu as pltpu
from jax.sharding import PartitionSpec as P

D = 1024
HD = 64
QH = 8
KVH = 2
NS = 128
HPD = 3

EPS = 1e-05
ROPE_BASE = 100000000000.0
HIGH = lax.Precision.HIGHEST
BF = jnp.bfloat16
F32 = jnp.float32

SX = 2 * NS
SQ = SX + HPD * HD
SZ = SQ + HD
SS = SZ + HPD * HD
SK = SS + HD
SV = SK + HD
WIDE = SV + HD


def dg(left, right, ca, cb, precision=None):
    return lax.dot_general(
        left, right, (((ca,), (cb,)), ((), ())), precision=precision, preferred_element_type=F32
    )


def product(left, right):
    return dg(left, right, 1, 0)


def against(left, right):
    return dg(left, right, 1, 1)


def outer(left, right):
    return dg(left, right, 0, 0)


def swap(value):
    return lax.ppermute(value, "col", [(0, 1), (1, 0)])


def flip(value, axis, step):
    count = lax.axis_size(axis)
    return lax.ppermute(value, axis, [(i, i ^ step) for i in range(count)])


def rope(value, cosine, sine):
    half = HD // 2
    turned = jnp.concatenate([-value[:, half:], value[:, :half]], axis=1)
    return value * cosine + turned * sine


def unrope(value, cosine, sine):
    half = HD // 2
    turned = jnp.concatenate([value[:, half:], -value[:, :half]], axis=1)
    return value * cosine + turned * sine


def spread(cols, width):
    rows = cols[0].shape[0]
    return jnp.concatenate([jnp.broadcast_to(c, (rows, width)) for c in cols], axis=1)


def head_sums(value):
    return [jnp.sum(value[:, h * HD : (h + 1) * HD], axis=1, keepdims=True) for h in range(HPD)]


def load_tokens(r, parts, whole, rows):
    whole[0:8, :] = jnp.zeros((8, whole.shape[1]), F32)
    for k in range(len(parts)):
        start = pl.multiple_of((r ^ k) * rows + 8, 8)
        whole[pl.ds(start, rows), :] = parts[k][...]


def filtered(whole, taps, first, rows):
    pre = taps[4:5, :] + whole[pl.ds(first + 5, rows), 0:SZ] * taps[0:1, :]
    for j in range(1, 4):
        pre = pre + whole[pl.ds(first + 5 + j, rows), 0:SZ] * taps[j : j + 1, :]
    return pre


def step_parts(whole, heads, first, rows, tri):
    raw = whole[pl.ds(first + 8, rows), SS:SK] + heads[0:1, :]
    step = jnp.maximum(raw, 0.0) + jnp.log1p(jnp.exp(-jnp.abs(raw)))
    logs = dg(tri, step * heads[1:2, :], 1, 0, HIGH)
    turned = jnp.transpose(jnp.concatenate([step, logs], axis=1))
    return raw, step, logs, turned


def masks(doc_col, doc_row, first, last, rows):
    dc = doc_col[pl.ds(first, rows), :]
    t = lax.broadcasted_iota(jnp.int32, (rows, last), 0) + first
    s = lax.broadcasted_iota(jnp.int32, (rows, last), 1)
    return (dc == doc_row[:, 0:last]) & (t >= s)


def forward_kernel(
    r_ref, p0, p1, p2, p3, cosine, sine, doc_col, doc_row, taps, heads, skip,
    feat, total, states, lse, whole, qs, ks, vs, state,
):
    r = r_ref[0]
    rows = p0.shape[0]
    chunks = 4
    load_tokens(r, (p0, p1, p2, p3), whole, rows)
    ti = lax.broadcasted_iota(jnp.int32, (rows, rows), 0)
    si = lax.broadcasted_iota(jnp.int32, (rows, rows), 1)
    tri = (ti >= si).astype(F32)
    state[...] = jnp.zeros_like(state)
    scale = HD ** (-0.5)
    for c in range(chunks):
        first = c * rows
        slot = r ^ c
        pre = filtered(whole, taps[...], first, rows)
        act = pre * jax.nn.sigmoid(pre)
        inject = act[:, 0:NS].astype(BF)
        read = act[:, NS : 2 * NS].astype(BF)
        inner_x = act[:, SX:SQ]
        raw, step, logs, turned = step_parts(whole, heads[...], first, rows, tri)
        dc = doc_col[pl.ds(first, rows), :]
        allowed = (dc == doc_row[:, first : first + rows]) & (ti >= si)
        dt = spread([step[:, h : h + 1] for h in range(HPD)], HD)
        lg = spread([logs[:, h : h + 1] for h in range(HPD)], HD)
        xd = (inner_x * dt).astype(BF)
        meet = against(read, inject)
        inner = []
        for h in range(HPD):
            gap = logs[:, h : h + 1] - turned[HD + h : HD + h + 1, :]
            decay = jnp.exp(jnp.where(allowed, gap, -1e30))
            inner.append(product((meet * decay).astype(BF), xd[:, h * HD : (h + 1) * HD]))
        inner = jnp.concatenate(inner, axis=1)
        old = state[...]
        states[c] = old
        end_doc = dc[rows - 1 : rows, :]
        last_doc = doc_col[first - 1 : first, :] if c else end_doc - 1
        keep = (dc == last_doc).astype(F32)
        carried = product(read, old.astype(BF)) * (jnp.exp(lg) * keep)
        tail = (dc == end_doc).astype(F32)
        end = lg[rows - 1 : rows, :]
        toward = jnp.exp(end - lg) * tail * dt
        going = jnp.exp(end) * (end_doc == last_doc).astype(F32)
        state[...] = old * going + outer(inject, (toward * inner_x).astype(BF))
        y = inner + carried + skip[...] * inner_x
        total[pl.ds(first, rows), :] = y
        z = whole[pl.ds(first + 8, rows), SZ:SS]
        gated = y * (z * jax.nn.sigmoid(z))
        cs = cosine[pl.ds(first, rows), :]
        sn = sine[pl.ds(first, rows), :]
        query = rope(whole[pl.ds(first + 8, rows), SQ:SZ], cs, sn).astype(BF)
        qs[pl.ds(first, rows), :] = query
        ks[pl.ds(first, rows), :] = rope(whole[pl.ds(first + 8, rows), SK:SV], cs, sn).astype(BF)
        vs[pl.ds(first, rows), :] = whole[pl.ds(first + 8, rows), SV:WIDE].astype(BF)
        last = first + rows
        score = jnp.where(
            masks(doc_col, doc_row, first, last, rows),
            against(query, ks[0:last, :]) * scale,
            -1e30,
        )
        peak = jnp.max(score, axis=1, keepdims=True)
        weight = jnp.exp(score - peak)
        bottom = jnp.sum(weight, axis=1, keepdims=True)
        att = product((weight / bottom).astype(BF), vs[0:last, :])
        lse[pl.ds(first, rows), :] = peak + jnp.log(bottom)
        feat[slot] = jnp.concatenate([gated, att], axis=1).astype(BF)


def backward_kernel(
    r_ref, p0, p1, p2, p3, dfeat, total, states, lse, cosine, sine, doc_col, doc_row, taps,
    heads, skip, dproj, small, whole, dpre, qs, ks, vs, dks, dvs, dstate,
):
    r = r_ref[0]
    rows = p0.shape[0]
    chunks = 4
    load_tokens(r, (p0, p1, p2, p3), whole, rows)
    ti = lax.broadcasted_iota(jnp.int32, (rows, rows), 0)
    si = lax.broadcasted_iota(jnp.int32, (rows, rows), 1)
    tri = (ti >= si).astype(F32)
    scale = HD ** (-0.5)
    small[...] = jnp.zeros_like(small)
    dstate[...] = jnp.zeros_like(dstate)
    dks[...] = jnp.zeros_like(dks)
    dvs[...] = jnp.zeros_like(dvs)
    dpre[chunks * rows :, :] = jnp.zeros((8, SZ), F32)
    for c in range(chunks):
        first = c * rows
        cs = cosine[pl.ds(first, rows), :]
        sn = sine[pl.ds(first, rows), :]
        qs[pl.ds(first, rows), :] = rope(whole[pl.ds(first + 8, rows), SQ:SZ], cs, sn).astype(BF)
        ks[pl.ds(first, rows), :] = rope(whole[pl.ds(first + 8, rows), SK:SV], cs, sn).astype(BF)
        vs[pl.ds(first, rows), :] = whole[pl.ds(first + 8, rows), SV:WIDE].astype(BF)
    for c in reversed(range(chunks)):
        first = c * rows
        last = first + rows
        slot = r ^ c
        datt = dfeat[slot, :, HPD * HD :]
        query = qs[pl.ds(first, rows), :]
        score = jnp.where(
            masks(doc_col, doc_row, first, last, rows),
            against(query, ks[0:last, :]) * scale,
            -1e30,
        )
        prob = jnp.exp(score - lse[pl.ds(first, rows), :])
        dprob = against(datt, vs[0:last, :])
        lean = jnp.sum(prob * dprob, axis=1, keepdims=True)
        dscore = (prob * (dprob - lean) * scale).astype(BF)
        dq = product(dscore, ks[0:last, :])
        dks[0:last, :] += outer(dscore, query)
        dvs[0:last, :] += outer(prob.astype(BF), datt)
        cs = cosine[pl.ds(first, rows), :]
        sn = sine[pl.ds(first, rows), :]
        dproj[slot, :, SQ:SZ] = unrope(dq, cs, sn).astype(BF)
        dproj[slot, :, SK:WIDE] = jnp.concatenate(
            [unrope(dks[pl.ds(first, rows), :], cs, sn), dvs[pl.ds(first, rows), :]], axis=1
        ).astype(BF)

        pre = filtered(whole, taps[...], first, rows)
        sig = jax.nn.sigmoid(pre)
        act = pre * sig
        inject = act[:, 0:NS].astype(BF)
        read = act[:, NS : 2 * NS].astype(BF)
        inner_x = act[:, SX:SQ]
        raw, step, logs, turned = step_parts(whole, heads[...], first, rows, tri)
        dc = doc_col[pl.ds(first, rows), :]
        allowed = (dc == doc_row[:, first:last]) & (ti >= si)
        dt = spread([step[:, h : h + 1] for h in range(HPD)], HD)
        lg = spread([logs[:, h : h + 1] for h in range(HPD)], HD)
        end_doc = dc[rows - 1 : rows, :]
        last_doc = doc_col[first - 1 : first, :] if c else end_doc - 1
        keep = (dc == last_doc).astype(F32)
        tail = (dc == end_doc).astype(F32)
        end = lg[rows - 1 : rows, :]
        going = jnp.exp(end) * (end_doc == last_doc).astype(F32)
        near = jnp.exp(end - lg) * tail
        toward = near * dt
        ek = jnp.exp(lg) * keep

        dgated = dfeat[slot, :, 0 : HPD * HD].astype(F32)
        z = whole[pl.ds(first + 8, rows), SZ:SS]
        zs = jax.nn.sigmoid(z)
        dz = dgated * total[pl.ds(first, rows), :] * (zs * (1.0 + z * (1.0 - zs)))
        dy = dgated * (z * zs)
        dyb = dy.astype(BF)
        small[6:7, 0 : HPD * HD] += jnp.sum(dy * inner_x, axis=0, keepdims=True)
        xd = (inner_x * dt).astype(BF)
        old = states[c]
        oldb = old.astype(BF)
        dst = dstate[...]
        dstb = dst.astype(BF)
        meet = against(read, inject)
        dmeet = jnp.zeros((rows, rows), F32)
        ahead = []
        behind = []
        dxt = []
        for h in range(HPD):
            gap = logs[:, h : h + 1] - turned[HD + h : HD + h + 1, :]
            decay = jnp.exp(jnp.where(allowed, gap, -1e30))
            mixed = meet * decay
            dyh = dyb[:, h * HD : (h + 1) * HD]
            dxt.append(outer(mixed.astype(BF), dyh))
            dmix = against(dyh, xd[:, h * HD : (h + 1) * HD])
            dmeet = dmeet + dmix * decay
            flow = dmix * mixed
            ahead.append(jnp.sum(flow, axis=1, keepdims=True))
            behind.append(jnp.sum(flow, axis=0, keepdims=True))
        dxt = jnp.concatenate(dxt, axis=1)
        behind = jnp.transpose(
            jnp.concatenate(behind + [jnp.zeros((128 - HPD, rows), F32)], axis=0)
        )
        v = product(inject, dstb)
        dx = skip[...] * dy + dt * dxt + toward * v
        pull = head_sums(inner_x * dxt)
        xv = inner_x * v
        push = head_sums(near * xv)
        send = toward * xv
        sends = head_sums(send)
        seen = head_sums(dy * (product(read, oldb) * ek))
        dyk = (dy * ek).astype(BF)
        dmeet = dmeet.astype(BF)
        dread = product(dmeet, inject) + against(dyk, oldb)
        dinject = outer(dmeet, read) + against((toward * inner_x).astype(BF), dstb)
        closing = jnp.sum(send, axis=0, keepdims=True) + jnp.sum(
            dst * old, axis=0, keepdims=True
        ) * going
        closing = head_sums(closing)
        dstate[...] = dst * going + outer(read, dyk)
        dlog = jnp.concatenate(
            [ahead[h] + seen[h] - sends[h] - behind[:, h : h + 1] for h in range(HPD)]
            + [jnp.zeros((rows, HD - HPD), F32)],
            axis=1,
        )
        ends = jnp.concatenate(closing + [jnp.zeros((1, HD - HPD), F32)], axis=1)
        dla = dg(tri, dlog, 0, 0, HIGH) + ends
        dstep = (
            jnp.concatenate(
                [pull[h] + push[h] for h in range(HPD)] + [jnp.zeros((rows, HD - HPD), F32)],
                axis=1,
            )
            + dla * heads[1:2, :]
        )
        draw = dstep * jax.nn.sigmoid(raw)
        lane = lax.broadcasted_iota(jnp.int32, (rows, HD), 1)
        draw = jnp.where(lane < HPD, draw, 0.0)
        small[5:6, 0:HD] += jnp.sum(draw, axis=0, keepdims=True)
        small[5:6, 128 : 128 + HD] += jnp.sum(dla * step, axis=0, keepdims=True) * heads[1:2, :]
        dproj[slot, :, SZ:SK] = jnp.concatenate([dz, draw], axis=1).astype(BF)
        dact = jnp.concatenate([dinject, dread, dx, jnp.zeros((rows, HD), F32)], axis=1)
        dpre[pl.ds(first, rows), :] = dact * (sig * (1.0 + pre * (1.0 - sig)))
    for c in range(chunks):
        first = c * rows
        slot = r ^ c
        here = dpre[pl.ds(first, rows), :]
        back = here * taps[3:4, :]
        small[4:5, :] += jnp.sum(here, axis=0, keepdims=True)
        for j in range(4):
            small[j : j + 1, :] += jnp.sum(
                here * whole[pl.ds(first + 5 + j, rows), 0:SZ], axis=0, keepdims=True
            )
            if j < 3:
                back = back + dpre[pl.ds(first + 3 - j, rows), :] * taps[j : j + 1, :]
        dproj[slot, :, 0:SQ] = back[:, 0:SQ].astype(BF)


def mix_forward(r, parts, tables):
    rows = parts[0].shape[0]
    length = 4 * rows
    vm = pl.BlockSpec(memory_space=pltpu.VMEM)
    return pl.pallas_call(
        forward_kernel,
        name="mix_forward",
        in_specs=[pl.BlockSpec(memory_space=pltpu.SMEM)] + [vm] * 11,
        out_specs=[vm] * 4,
        out_shape=[
            jax.ShapeDtypeStruct((4, rows, HPD * HD + HD), BF),
            jax.ShapeDtypeStruct((length, HPD * HD), F32),
            jax.ShapeDtypeStruct((4, NS, HPD * HD), F32),
            jax.ShapeDtypeStruct((length, 1), F32),
        ],
        scratch_shapes=[
            pltpu.VMEM((length + 8, WIDE), F32),
            pltpu.VMEM((length, HD), BF),
            pltpu.VMEM((length, HD), BF),
            pltpu.VMEM((length, HD), BF),
            pltpu.VMEM((NS, HPD * HD), F32),
        ],
        cost_estimate=pl.CostEstimate(
            flops=2 * 10**9, bytes_accessed=6 * 10**6, transcendentals=2 * 10**6
        ),
        compiler_params=pltpu.CompilerParams(vmem_limit_bytes=60 * 2**20),
    )(r, *parts, *tables)


def mix_backward(r, parts, dfeat, total, states, lse, tables):
    rows = parts[0].shape[0]
    length = 4 * rows
    vm = pl.BlockSpec(memory_space=pltpu.VMEM)
    return pl.pallas_call(
        backward_kernel,
        name="mix_backward",
        in_specs=[pl.BlockSpec(memory_space=pltpu.SMEM)] + [vm] * 15,
        out_specs=[vm] * 2,
        out_shape=[
            jax.ShapeDtypeStruct((4, rows, WIDE), BF),
            jax.ShapeDtypeStruct((8, SZ), F32),
        ],
        scratch_shapes=[
            pltpu.VMEM((length + 8, WIDE), F32),
            pltpu.VMEM((length + 8, SZ), F32),
            pltpu.VMEM((length, HD), BF),
            pltpu.VMEM((length, HD), BF),
            pltpu.VMEM((length, HD), BF),
            pltpu.VMEM((length, HD), F32),
            pltpu.VMEM((length, HD), F32),
            pltpu.VMEM((NS, HPD * HD), F32),
        ],
        cost_estimate=pl.CostEstimate(
            flops=5 * 10**9, bytes_accessed=9 * 10**6, transcendentals=2 * 10**6
        ),
        compiler_params=pltpu.CompilerParams(vmem_limit_bytes=60 * 2**20),
    )(r, *parts, dfeat, total, states, lse, *tables)


def row_spread(block):
    return [block] + [flip(block, "row", k) for k in range(1, 4)]


def row_sum(parts):
    held = parts[0]
    for k in (3, 1, 2):
        held = held + flip(parts[k].astype(BF), "row", k).astype(F32)
    return held


def tree_sum(value, axis):
    step = 1
    while step < lax.axis_size(axis):
        value = value + flip(value, axis, step)
        step *= 2
    return value


def dp_sum(value):
    count = lax.axis_size("dp")
    me = lax.axis_index("dp")
    steps = []
    step = 1
    while step < count:
        steps.append(step)
        step *= 2
    for step in steps:
        half = value.shape[0] // 2
        high = ((me // step) % 2).astype(jnp.int32)
        keep = lax.dynamic_slice_in_dim(value, high * half, half, 0)
        give = lax.dynamic_slice_in_dim(value, (1 - high) * half, half, 0)
        value = (keep.astype(F32) + flip(give, "dp", step).astype(F32)).astype(BF)
    for step in reversed(steps):
        high = (me // step) % 2
        got = flip(value, "dp", step)
        value = jnp.where(
            high == 0,
            jnp.concatenate([value, got], axis=0),
            jnp.concatenate([got, value], axis=0),
        )
    return value


def on_device(
    block_input,
    output_grad,
    document_ids,
    mixer_gain,
    mamba_gate,
    mamba_input,
    mamba_step,
    query_weight,
    key_weight,
    value_weight,
    state_weight,
    input_filter,
    input_shift,
    state_filter,
    state_shift,
    step_bias,
    decay_log,
    skip_gain,
    mixer_out,
    feed_gain,
    feed_gate,
    feed_up,
    feed_down,
):
    length = document_ids.shape[1]
    row = lax.axis_index("row")
    col = lax.axis_index("col")
    pair_head = (row * lax.axis_size("col") + col) // (QH // KVH)
    r = jnp.reshape(row, (1,)).astype(jnp.int32)
    mixer_scale = mixer_gain.astype(F32)
    feed_scale = feed_gain.astype(F32)

    def mine(weight, which, axis):
        half = weight.shape[axis] // 2
        return lax.dynamic_slice_in_dim(weight, which * half, half, axis)

    def joint(which):
        step = mine(mamba_step, which, 1)
        return jnp.concatenate(
            [
                state_weight,
                mine(mamba_input, which, 1),
                mine(query_weight, which, 1),
                mine(mamba_gate, which, 1),
                jnp.pad(step, ((0, 0), (0, HD - step.shape[1]))),
                lax.dynamic_slice_in_dim(key_weight, pair_head * HD, HD, 1),
                lax.dynamic_slice_in_dim(value_weight, pair_head * HD, HD, 1),
            ],
            axis=1,
        )

    residual = block_input.astype(F32)
    square = jnp.sum(residual * residual, axis=1)
    inverse_one = lax.rsqrt((square + swap(square)) / D + EPS)[:, None]
    normed_one = (residual * inverse_one * mixer_scale).astype(BF)
    ones = row_spread(normed_one)
    joint_own = joint(col)
    joint_send = joint(1 - col)
    joint_got = swap(joint_send)
    feed_own = jnp.concatenate([mine(feed_gate, col, 1), mine(feed_up, col, 1)], axis=1)
    feed_send = jnp.concatenate([mine(feed_gate, 1 - col, 1), mine(feed_up, 1 - col, 1)], axis=1)
    feed_got = swap(feed_send)
    parts = []
    for k in range(4):
        parts.append(product(ones[k], joint_own) + product(swap(ones[k]), joint_got))

    half = HD // 2
    place = jnp.arange(length).astype(F32)
    rates = ROPE_BASE ** (-2.0 * jnp.arange(half).astype(F32) / HD)
    angle = place[:, None] * rates[None, :]
    cosine = jnp.concatenate([jnp.cos(angle)] * 2, axis=1)
    sine = jnp.concatenate([jnp.sin(angle)] * 2, axis=1)
    taps = jnp.concatenate(
        [
            jnp.concatenate([state_filter, state_shift[:, None]], axis=1),
            jnp.concatenate([input_filter, input_shift[:, None]], axis=1),
            jnp.zeros((HD, 5), BF),
        ],
        axis=0,
    ).astype(F32).T
    taps = jnp.pad(taps, ((0, 3), (0, 0)))
    heads = jnp.pad(
        jnp.stack([step_bias.astype(F32), -jnp.exp(decay_log.astype(F32))]),
        ((0, 6), (0, HD - HPD)),
    )
    skip = jnp.repeat(skip_gain.astype(F32), HD)[None, :]
    tables = (
        cosine,
        sine,
        document_ids.reshape(length, 1),
        document_ids.reshape(1, length),
        taps,
        heads,
        skip,
    )
    feat, total, states, lse = mix_forward(r, parts, tables)
    feat_got = swap(feat)
    grads = row_spread(output_grad)

    out_own = mine(mixer_out, col, 0)
    out_other = mine(mixer_out, 1 - col, 0)
    after_mixer = residual + row_sum(
        [product(feat[k], out_own) + product(feat_got[k], out_other) for k in range(4)]
    )
    square = jnp.sum(after_mixer * after_mixer, axis=1)
    inverse_two = lax.rsqrt((square + swap(square)) / D + EPS)[:, None]
    normed_two = (after_mixer * inverse_two * feed_scale).astype(BF)
    twos = row_spread(normed_two)

    down_own = mine(feed_down, col, 0)
    down_other = mine(feed_down, 1 - col, 0)
    wide = feed_own.shape[1] // 2
    hidden = []
    edges = []
    hidden_got = []
    edges_got = []
    backs = []
    for k in range(4):
        both = product(twos[k], feed_own) + product(swap(twos[k]), feed_got)
        gate = both[:, :wide]
        upper = both[:, wide:]
        sigma = jax.nn.sigmoid(gate)
        hidden.append((gate * sigma * upper).astype(BF))
        given = against(grads[k], down_own) + swap(against(grads[k], down_other).astype(BF)).astype(
            F32
        )
        edge = jnp.concatenate(
            [
                given * upper * (sigma * (1.0 + gate * (1.0 - sigma))),
                given * (gate * sigma),
            ],
            axis=1,
        ).astype(BF)
        got = swap(edge)
        edges.append(edge)
        edges_got.append(got)
        backs.append(against(edge, feed_own) + against(got, feed_send))
    feed_back = row_sum(backs)
    scaled = feed_back * feed_scale
    inner = jnp.sum(scaled * after_mixer, axis=1)
    inner = (inner + swap(inner))[:, None]
    feed_gain_grad = jnp.sum(feed_back * after_mixer * inverse_two, axis=0)
    mixer_grad = (
        output_grad.astype(F32)
        + inverse_two * scaled
        - after_mixer * (inverse_two**3 * inner / D)
    )
    mixer_low = mixer_grad.astype(BF)
    lows = row_spread(mixer_low)
    dfeat = jnp.stack(
        [
            (
                against(low, out_own) + swap(against(low, out_other).astype(BF)).astype(F32)
            ).astype(BF)
            for low in lows
        ]
    )

    hidden_got = [swap(h) for h in hidden]
    block_output = after_mixer + row_sum(
        [product(hidden[k], down_own) + product(hidden_got[k], down_other) for k in range(4)]
    )
    twos_all = jnp.concatenate(twos, axis=0)
    grads_all = jnp.concatenate(grads, axis=0)
    feed_wgrad = jnp.concatenate(
        [
            outer(twos_all, jnp.concatenate(edges, axis=0)),
            outer(twos_all, jnp.concatenate(edges_got, axis=0)),
            jnp.concatenate(
                [
                    outer(jnp.concatenate(hidden, axis=0), grads_all),
                    outer(jnp.concatenate(hidden_got, axis=0), grads_all),
                ],
                axis=0,
            ),
        ],
        axis=1,
    ).astype(BF)
    feed_sum = dp_sum(feed_wgrad).astype(F32)

    def ordered(own, got, axis):
        return jnp.where(
            col == 0,
            jnp.concatenate([own, got], axis=axis),
            jnp.concatenate([got, own], axis=axis),
        )

    gate_wgrad = ordered(feed_sum[:, 0:wide], feed_sum[:, 2 * wide : 3 * wide], 1)
    upper_wgrad = ordered(feed_sum[:, wide : 2 * wide], feed_sum[:, 3 * wide : 4 * wide], 1)
    down_sum = feed_sum[:, 4 * wide :]
    down_half = down_sum.shape[0] // 2
    down_wgrad = ordered(down_sum[:down_half], down_sum[down_half:], 0)

    lows_all = jnp.concatenate(lows, axis=0)
    flat = feat.shape[2]
    out_sum = dp_sum(
        jnp.concatenate(
            [
                outer(feat.reshape(length, flat), lows_all),
                outer(feat_got.reshape(length, flat), lows_all),
            ],
            axis=0,
        ).astype(BF)
    ).astype(F32)
    out_wgrad = ordered(out_sum[:flat], out_sum[flat:], 0)

    dproj, small = mix_backward(r, parts, dfeat, total, states, lse, tables)
    dproj_got = swap(dproj)
    mixer_back = row_sum(
        [against(dproj[k], joint_own) + against(dproj_got[k], joint_send) for k in range(4)]
    )
    scaled = mixer_back * mixer_scale
    inner = jnp.sum(scaled * residual, axis=1)
    inner = (inner + swap(inner))[:, None]
    mixer_gain_grad = jnp.sum(mixer_back * residual * inverse_one, axis=0)
    input_grad = mixer_grad + (
        inverse_one * scaled - residual * (inverse_one**3 * inner / D)
    )

    ones_all = jnp.concatenate(ones, axis=0)
    own_wgrad = outer(ones_all, dproj.reshape(length, WIDE))
    got_wgrad = outer(ones_all, dproj_got.reshape(length, WIDE))
    mix_sum = dp_sum(
        jnp.concatenate([own_wgrad[:, SX:SK], got_wgrad[:, SX:SK]], axis=1).astype(BF)
    ).astype(F32)
    span = SK - SX

    def pick(start, stop):
        return ordered(
            mix_sum[:, start - SX : stop - SX],
            mix_sum[:, span + start - SX : span + stop - SX],
            1,
        )

    shared = own_wgrad + got_wgrad
    pair = shared[:, SK:WIDE]
    blank = jnp.zeros_like(pair)
    shared = jnp.concatenate(
        [
            shared[:, 0:SX],
            jnp.where(pair_head == 0, pair, blank),
            jnp.where(pair_head == 1, pair, blank),
        ],
        axis=1,
    ).astype(BF)
    deep = shared.shape[0] // 4
    shared = row_sum(
        [
            lax.dynamic_slice_in_dim(shared, (row ^ k) * deep, deep, 0).astype(F32)
            for k in range(4)
        ]
    ).astype(BF)
    shared = dp_sum(shared)
    pieces = row_spread(shared)
    shared = jnp.zeros((4 * deep, shared.shape[1]), BF)
    for k in range(4):
        shared = lax.dynamic_update_slice_in_dim(shared, pieces[k], (row ^ k) * deep, 0)
    shared = shared.astype(F32)
    state_wgrad = shared[:, 0:SX]
    key_wgrad = jnp.concatenate(
        [shared[:, SX : SX + HD], shared[:, SX + 2 * HD : SX + 3 * HD]], axis=1
    )
    value_wgrad = jnp.concatenate(
        [shared[:, SX + HD : SX + 2 * HD], shared[:, SX + 3 * HD : SX + 4 * HD]], axis=1
    )

    small = tree_sum(small, "dp")
    filters = small[0:5, :]
    wide_small = jnp.concatenate(
        [
            jnp.pad(filters[:, 0:SX], ((0, 0), (0, D // 2 - SX))),
            jnp.zeros((3, D // 2), F32),
        ],
        axis=0,
    )
    wide_small = wide_small + swap(wide_small)
    gains = tree_sum(jnp.stack([mixer_gain_grad, feed_gain_grad]), "dp")
    wide_small = tree_sum(jnp.concatenate([wide_small[0:6], gains], axis=0), "row")
    state_filters = wide_small[0:5, 0:SX]
    input_filters = filters[:, SX:SQ]
    skip_wgrad = jnp.sum(small[6, 0 : HPD * HD].reshape(HPD, HD), axis=1)
    return (
        block_output,
        input_grad,
        wide_small[6],
        pick(SZ, SS),
        pick(SX, SQ),
        pick(SS, SS + HPD),
        pick(SQ, SZ),
        key_wgrad,
        value_wgrad,
        state_wgrad,
        input_filters[0:4].T,
        input_filters[4],
        state_filters[0:4].T,
        state_filters[4],
        small[5, 0:HPD],
        small[5, 128 : 128 + HPD],
        skip_wgrad,
        out_wgrad,
        wide_small[7],
        gate_wgrad,
        upper_wgrad,
        down_wgrad,
    )


def solution(mesh):
    tokens = P(("dp", "row"), "col")
    heads = P(("row", "col"))
    placed = (
        tokens,
        tokens,
        P("dp", None),
        P("col"),
        P("col", "row"),
        P("col", "row"),
        P("col", "row"),
        P("col", "row"),
        P("col", None),
        P("col", None),
        P("col", None),
        P(("row", "col"), None),
        heads,
        P(),
        P(),
        heads,
        heads,
        heads,
        P("row", "col"),
        P("col"),
        P("col", "row"),
        P("col", "row"),
        P("row", "col"),
    )
    return jax.shard_map(
        on_device,
        mesh=mesh,
        in_specs=placed,
        out_specs=(
            tokens,
            tokens,
            P("col"),
            P("col", "row"),
            P("col", "row"),
            P("col", "row"),
            P("col", "row"),
            P("col", None),
            P("col", None),
            P("col", None),
            P(("row", "col"), None),
            heads,
            P(),
            P(),
            heads,
            heads,
            heads,
            P("row", "col"),
            P("col"),
            P("col", "row"),
            P("col", "row"),
            P("row", "col"),
        ),
        check_vma=False,
    )
```

time: 930 us -> 402 us (0.43)
  waiting for transfers between devices: 425 us -> 168 us
  local copies, waits for them, and re-layouts: 120 us -> 25 us
  other arithmetic: 123 us -> 31.3 us
  blocking collectives: 88.1 us -> 0 us
  matrix products: 137 us -> 62.1 us
  starting transfers between devices: 1.76 us -> 68.3 us
  Pallas kernels: 0 us -> 39.7 us
  between operations: 16.8 us -> 2.71 us
  loops' own time: 11.8 us -> 0 us
    psum x3 -> x0, waiting for transfers between devices: 173 us -> none  [the longest x1 103 us: on_device(): lax.psum((mixer_gain_grad, key_wgrad, value_wgrad, state_wgrad, state_fil...]
    ppermute x0 -> x85, waiting for transfers between devices: none -> 168 us  [the longest x52 167 us: flip(): return lax.ppermute(value, axis, [(i, i ^ step) for i in range(count)])]
    all_gather x9 -> x0, waiting for transfers between devices: 135 us -> none  [the longest x4 103 us: row_tokens(): return lax.all_gather(values, 'row', axis=0, tiled=True)]
    reduce_scatter x11 -> x0, waiting for transfers between devices: 115 us -> none  [the longest x4 76.9 us: row_out(): lax.psum_scatter(term(jnp.int32(0), lax.axis_size('row') * rows).astype(j...]
    psum x6 -> x0, blocking collectives: 72.8 us -> none  [the longest x1 42.7 us: on_device(): lax.psum((mixer_gain_grad, key_wgrad, value_wgrad, state_wgrad, state_fil...]
    dot_general x90 -> x72, matrix products: 131 us -> 62.1 us  [dg(): lax.dot_general(left, right, (((ca,), (cb,)), ((), ())), precision=precis...]
    ppermute x0 -> x85, starting transfers between devices: none -> 68.3 us  [the longest x52 61.2 us: flip(): return lax.ppermute(value, axis, [(i, i ^ step) for i in range(count)])]
    dynamic_update_slice x30 -> x3, local copies, waits for them, and re-layouts: 44.5 us -> 0.05 us  [on_device(): lax.dynamic_update_slice_in_dim(shared, pieces[k], (row ^ k) * deep, 0)]
  transfers between devices with their start and end apart: 23 -> 85, of which waited for: 18 -> 28; matrix products, arithmetic and copies ran while one was open for 20% -> 28% of each run, Pallas kernels for 0% -> 10%
where the time goes in v1:
time: 402 us; the launch traced here: 397 us
  waiting for transfers between devices  168 us (42%)
  starting transfers between devices  68.3 us (17%)
  matrix products  62.1 us (15%)
  Pallas kernels  39.7 us (10%)
  other arithmetic  31.3 us (8%)
  local copies, waits for them, and re-layouts  25 us (6%)
    ppermute x52, waiting for transfers between devices, flip(): return lax.ppermute(value, axis, [(i, i ^ step) for i in range(count)])  167 us
    dot_general x72, matrix products, dg(): lax.dot_general(left, right, (((ca,), (cb,)), ((), ())), precision=precis...  62.1 us
    ppermute x52, starting transfers between devices, flip(): return lax.ppermute(value, axis, [(i, i ^ step) for i in range(count)])  61.2 us
    pallas_call x1, Pallas kernels, mix_backward(): pl.pallas_call(backward_kernel, name='mix_backward', in_specs=[pl.BlockSp...  27.9 us
    pallas_call x1, Pallas kernels, mix_forward(): pl.pallas_call(forward_kernel, name='mix_forward', in_specs=[pl.BlockSpec...  11.8 us
    select_n x8, other arithmetic, ordered(): jnp.where(col == 0, jnp.concatenate([own, got], axis=axis), jnp.concatena...  8.6 us
  transfers between devices with their start and end apart: 85, of which 28 were waited for; matrix products, arithmetic and copies ran while one was open for 28% of the time, Pallas kernels for 10%

profile of v1, /device:TPU:0, one launch (start us, length us, event | category | flops | bytes accessed | tf_op | source)
XLA Modules:
  0.0 396.9 jit_solution(12874532979823440282)
XLA Ops:
  0.7 3.0 collective-permute-start.35
  3.7 1.5 collective-permute-start.31
  6.4 1.9 fusion.33
  8.8 1.7 constant_dynamic-update-slice_fusion.7
  20.1 1.9 multiply_sine_fusion
  27.3 2.5 concatenate.194
  29.8 2.8 concatenate.193
  34.5 1.9 fusion.35
  36.4 2.9 collective-permute-start.7
  39.3 1.9 fusion.34
  42.9 3.0 collective-permute-done.7
  45.9 1.7 collective-permute-start.3
  48.0 3.4 collective-permute-done.5
  51.9 1.6 collective-permute-done.3
  61.1 11.8 %mix_forward.1 = (bf16[4,256,256]{2,1,0:T(8,128)(2,1)}, f32[1024,192]{1,0:T(8,128)}, f32[4,128,192]{2,1,0:T(8,128)}, f32[1024,1]{1,0:T(8,128)}) custom-call(s32[1]{0:T(128)} %bitcast.r_ref, f32[256,896]{1,0:T(8,128)} %convolution_add_fusion.3.p0, f32[256,896]{1,0:T(8,128)} %convolution_add_fusion.2.p1, f32[256,896]{1,0:T(8,128)} %convolution_add_fusion.1.p2, ...), custom_call_target="tpu_custom_call" | custom-call | flops 2000000000 | bytes 6000000 | tf_op jit(solution)/shard_map/mix_forward/pallas_call | solution.py:336
  74.2 1.5 fusion.111
  77.3 2.4 collective-permute-start.10
  82.7 4.8 %collective-permute-done.10 = bf16[256,512]{1,0:T(8,128)(2,1)S(1)} collective-permute-done((bf16[256,512]{1,0:T(8,128)(2,1)S(1)}, bf16[256,512]{1,0:T(8,128)(2,1)S(1)}, u32[]{:S(2)}, u32[]{:S(2)}) %collective-permute-start.10) | collective-permute-done | bytes 262176 | tf_op jit(solution)/shard_map/ppermute | solution.py:54
  87.5 5.0 %collective-permute-done.11 = bf16[256,512]{1,0:T(8,128)(2,1)S(1)} collective-permute-done((bf16[256,512]{1,0:T(8,128)(2,1)S(1)}, bf16[256,512]{1,0:T(8,128)(2,1)S(1)}, u32[]{:S(2)}, u32[]{:S(2)}) %collective-permute-start.11) | collective-permute-done | bytes 262176 | tf_op jit(solution)/shard_map/ppermute | solution.py:54
  96.5 1.5 collective-permute-start.21
  101.9 9.3 %collective-permute-done.17 = bf16[256,512]{1,0:T(8,128)(2,1)S(1)} collective-permute-done((bf16[256,512]{1,0:T(8,128)(2,1)S(1)}, bf16[256,512]{1,0:T(8,128)(2,1)S(1)}, u32[]{:S(2)}, u32[]{:S(2)}) %collective-permute-start.17) | collective-permute-done | bytes 262176 | tf_op jit(solution)/shard_map/ppermute | solution.py:54
  113.0 5.9 %collective-permute-done.25 = bf16[256,512]{1,0:T(8,128)(2,1)S(1)} collective-permute-done((bf16[256,512]{1,0:T(8,128)(2,1)S(1)}, bf16[256,512]{1,0:T(8,128)(2,1)S(1)}, u32[]{:S(2)}, u32[]{:S(2)}) %collective-permute-start.25) | collective-permute-done | bytes 262176 | tf_op jit(solution)/shard_map/ppermute | solution.py:54
  136.8 2.5 collective-permute-start.34
  142.1 12.7 %collective-permute-done.34 = bf16[256,512]{1,0:T(8,128)(2,1)S(1)} collective-permute-done((bf16[256,512]{1,0:T(8,128)(2,1)S(1)}, bf16[256,512]{1,0:T(8,128)(2,1)S(1)}, u32[]{:S(2)}, u32[]{:S(2)}) %collective-permute-start.34) | collective-permute-done | bytes 262176 | tf_op jit(solution)/shard_map/ppermute | solution.py:54
  155.4 3.3 collective-permute-done.38
  160.3 1.6 collective-permute-start.81
  162.1 2.5 collective-permute-start.49
  167.4 4.8 %collective-permute-done.49 = bf16[256,512]{1,0:T(8,128)(2,1)S(1)} collective-permute-done((bf16[256,512]{1,0:T(8,128)(2,1)S(1)}, bf16[256,512]{1,0:T(8,128)(2,1)S(1)}, u32[]{:S(2)}, u32[]{:S(2)}) %collective-permute-start.49) | collective-permute-done | bytes 262176 | tf_op jit(solution)/shard_map/ppermute | solution.py:54
  172.6 4.5 %collective-permute-done.47 = bf16[256,512]{1,0:T(8,128)(2,1)S(1)} collective-permute-done((bf16[256,512]{1,0:T(8,128)(2,1)S(1)}, bf16[256,512]{1,0:T(8,128)(2,1)S(1)}, u32[]{:S(2)}, u32[]{:S(2)}) %collective-permute-start.47) | collective-permute-done | bytes 262176 | tf_op jit(solution)/shard_map/ppermute | solution.py:54
  182.5 27.9 %mix_backward.1 = (bf16[4,256,896]{2,1,0:T(8,128)(2,1)}, f32[8,512]{1,0:T(8,128)}) custom-call(s32[1]{0:T(128)} %bitcast.r_ref, f32[256,896]{1,0:T(8,128)} %convolution_add_fusion.3.p0, f32[256,896]{1,0:T(8,128)} %convolution_add_fusion.2.p1, f32[256,896]{1,0:T(8,128)} %convolution_add_fusion.1.p2, f32[256,896]{1,0:T(8,128)} %convolution_add_fusion.p3, ...), custom_call_target="tpu_custom_call" | custom-call | flops 5000000000 | bytes 9000000 | tf_op jit(solution)/shard_map/mix_backward/pallas_call | solution.py:365
  210.4 1.6 collective-permute-start.56
  212.0 2.3 fusion.88
  214.3 2.3 fusion.90
  216.6 2.4 fusion.92
  219.0 2.7 collective-permute-start.57
  225.1 2.6 collective-permute-start.82
  230.1 18.2 %collective-permute-done.82 = bf16[128,1536]{1,0:T(8,128)(2,1)S(1)} collective-permute-done((bf16[128,1536]{1,0:T(8,128)(2,1)S(1)}, bf16[128,1536]{1,0:T(8,128)(2,1)S(1)}, u32[]{:S(2)}, u32[]{:S(2)}) %collective-permute-start.82) | collective-permute-done | bytes 393248 | tf_op jit(solution)/shard_map/ppermute | solution.py:54
  248.5 13.9 %collective-permute-done.78 = bf16[128,512]{1,0:T(8,128)(2,1)S(1)} collective-permute-done((bf16[128,512]{1,0:T(8,128)(2,1)S(1)}, bf16[128,512]{1,0:T(8,128)(2,1)S(1)}, u32[]{:S(2)}, u32[]{:S(2)}) %collective-permute-start.78) | collective-permute-done | bytes 131104 | tf_op jit(solution)/shard_map/ppermute | solution.py:54
  263.3 10.2 %collective-permute-done.79 = bf16[128,512]{1,0:T(8,128)(2,1)S(1)} collective-permute-done((bf16[128,512]{1,0:T(8,128)(2,1)S(1)}, bf16[128,512]{1,0:T(8,128)(2,1)S(1)}, u32[]{:S(2)}, u32[]{:S(2)}) %collective-permute-start.79) | collective-permute-done | bytes 131104 | tf_op jit(solution)/shard_map/ppermute | solution.py:54
  273.8 2.1 collective-permute-start.84
  277.1 5.7 %collective-permute-done.80 = bf16[256,512]{1,0:T(8,128)(2,1)S(1)} collective-permute-done((bf16[256,512]{1,0:T(8,128)(2,1)S(1)}, bf16[256,512]{1,0:T(8,128)(2,1)S(1)}, u32[]{:S(2)}, u32[]{:S(2)}) %collective-permute-start.80) | collective-permute-done | bytes 262176 | tf_op jit(solution)/shard_map/ppermute | solution.py:54
  284.2 14.6 %collective-permute-done.84 = bf16[256,1536]{1,0:T(8,128)(2,1)} collective-permute-done((bf16[256,1536]{1,0:T(8,128)(2,1)S(1)}, bf16[256,1536]{1,0:T(8,128)(2,1)}, u32[]{:S(2)}, u32[]{:S(2)}) %collective-permute-start.84) | collective-permute-done | bytes 786464 | tf_op jit(solution)/shard_map/ppermute | solution.py:54
  298.8 1.8 fusion
  304.4 1.6 fusion.15
  306.0 2.4 collective-permute-start.52
  310.6 2.8 fusion.106
  313.4 2.8 fusion.222
  316.4 1.5 collective-permute-start.67
  317.9 1.5 collective-permute-start.69
  321.5 2.6 collective-permute-done.67
  324.1 1.7 collective-permute-start.54
  328.1 3.2 collective-permute-done.70
  331.5 1.8 fusion.70
  333.6 5.1 %collective-permute-done.71 = bf16[32,512]{1,0:T(8,128)(2,1)S(1)} collective-permute-done((bf16[32,512]{1,0:T(8,128)(2,1)S(1)}, bf16[32,512]{1,0:T(8,128)(2,1)S(1)}, u32[]{:S(2)}, u32[]{:S(2)}) %collective-permute-start.71) | collective-permute-done | bytes 32800 | tf_op jit(solution)/shard_map/ppermute | solution.py:54
  338.7 3.4 collective-permute-start.72
  342.4 1.8 collective-permute-done.72
  344.4 2.4 collective-permute-done.60
  346.8 1.5 collective-permute-start.61
  348.3 2.3 collective-permute-done.61
  352.8 1.6 collective-permute-done.62
  358.6 6.0 %collective-permute-done.64 = bf16[128,1024]{1,0:T(8,128)(2,1)S(1)} collective-permute-done((bf16[128,1024]{1,0:T(8,128)(2,1)S(1)}, bf16[128,1024]{1,0:T(8,128)(2,1)S(1)}, u32[]{:S(2)}, u32[]{:S(2)}) %collective-permute-start.64) | collective-permute-done | bytes 262176 | tf_op jit(solution)/shard_map/ppermute | solution.py:54
  366.0 2.0 collective-permute-start.76
  368.0 9.1 %collective-permute-done.65 = bf16[128,1024]{1,0:T(8,128)(2,1)S(1)} collective-permute-done((bf16[128,1024]{1,0:T(8,128)(2,1)S(1)}, bf16[128,1024]{1,0:T(8,128)(2,1)S(1)}, u32[]{:S(2)}, u32[]{:S(2)}) %collective-permute-start.65) | collective-permute-done | bytes 262176 | tf_op jit(solution)/shard_map/ppermute | solution.py:54
  380.0 11.1 %collective-permute-done.66 = bf16[256,1024]{1,0:T(8,128)(2,1)S(1)} collective-permute-done((bf16[256,1024]{1,0:T(8,128)(2,1)S(1)}, bf16[256,1024]{1,0:T(8,128)(2,1)S(1)}, u32[]{:S(2)}, u32[]{:S(2)}) %collective-permute-start.66) | collective-permute-done | bytes 524320 | tf_op jit(solution)/shard_map/ppermute | solution.py:54
  (385 shorter events, 112.3 us)
Async XLA Ops:
  0.7 33.3 %collective-permute-start.35 = (bf16[256,512]{1,0:T(8,128)(2,1)}, bf16[256,512]{1,0:T(8,128)(2,1)}, u32[]{:S(2)}, u32[]{:S(2)}) collective-permute-start(bf16[256,512]{1,0:T(8,128)(2,1)} %param.24), channel_id=1, source_target_pairs={{0,2},{2,0},{4,6},{6,4},{1,3},{3,1},{5,7},{7,5},{8,10},{10,8},{12,... | collective-permute-start | bytes 786440 | tf_op jit(solution)/shard_map/ppermute | solution.py:54
  3.7 32.7 %collective-permute-start.31 = (bf16[256,512]{1,0:T(8,128)(2,1)}, bf16[256,512]{1,0:T(8,128)(2,1)}, u32[]{:S(2)}, u32[]{:S(2)}) collective-permute-start(bf16[256,512]{1,0:T(8,128)(2,1)} %param.24), channel_id=1, source_target_pairs={{0,6},{2,4},{4,2},{6,0},{1,7},{3,5},{5,3},{7,1},{8,14},{10,12},{12... | collective-permute-start | bytes 786440 | tf_op jit(solution)/shard_map/ppermute | solution.py:54
  5.2 36.0 %collective-permute-start.39 = (bf16[256,512]{1,0:T(8,128)(2,1)}, bf16[256,512]{1,0:T(8,128)(2,1)}, u32[]{:S(2)}, u32[]{:S(2)}) collective-permute-start(bf16[256,512]{1,0:T(8,128)(2,1)} %param.24), channel_id=1, source_target_pairs={{0,4},{2,6},{4,0},{6,2},{1,5},{3,7},{5,1},{7,3},{8,12},{10,14},{12... | collective-permute-start | bytes 786440 | tf_op jit(solution)/shard_map/ppermute | solution.py:54
  6.3 26.2 %collective-permute-start = (f32[256]{0:T(256)S(1)}, f32[256]{0:T(256)}, u32[]{:S(2)}, u32[]{:S(2)}) collective-permute-start(f32[256]{0:T(256)S(1)} %fusion.63), channel_id=1, source_target_pairs={{0,1},{1,0},{2,3},{3,2},{4,5},{5,4},{6,7},{7,6},{8,9},{9,8},{10,11... | collective-permute-start | bytes 3080 | tf_op jit(solution)/shard_map/ppermute | solution.py:49
  8.3 91.1 %collective-permute-start.29 = (bf16[256,256]{1,0:T(8,128)(2,1)}, bf16[256,256]{1,0:T(8,128)(2,1)}, u32[]{:S(2)}, u32[]{:S(2)}) collective-permute-start(bf16[256,256]{1,0:T(8,128)(2,1)} %fusion.33), channel_id=1, source_target_pairs={{0,1},{1,0},{2,3},{3,2},{4,5},{5,4},{6,7},{7,6},{8,9},{9,8},{10,11... | collective-permute-start | bytes 393224 | tf_op jit(solution)/shard_map/ppermute | solution.py:49
  32.6 22.6 %collective-permute-start.2 = (bf16[512,896]{1,0:T(8,128)(2,1)S(1)}, bf16[512,896]{1,0:T(8,128)(2,1)S(1)}, u32[]{:S(2)}, u32[]{:S(2)}) collective-permute-start(bf16[512,896]{1,0:T(8,128)(2,1)S(1)} %concatenate.194), channel_id=1, source_target_pairs={{0,1},{1,0},{2,3},{3,2},{4,5},{5,4},{6,7},{7,6},{8,9},{9,8},{10,11... | collective-permute-start | bytes 2752520 | tf_op jit(solution)/shard_map/ppermute | solution.py:49
  33.9 62.2 %collective-permute-start.15 = (bf16[512,512]{1,0:T(8,128)(2,1)}, bf16[512,512]{1,0:T(8,128)(2,1)}, u32[]{:S(2)}, u32[]{:S(2)}) collective-permute-start(bf16[512,512]{1,0:T(8,128)(2,1)} %pad_maximum_fusion.6), channel_id=1, source_target_pairs={{0,1},{1,0},{2,3},{3,2},{4,5},{5,4},{6,7},{7,6},{8,9},{9,8},{10,11... | collective-permute-start | bytes 1572872 | tf_op jit(solution)/shard_map/ppermute | solution.py:49
  36.4 9.5 %collective-permute-start.7 = (bf16[256,512]{1,0:T(8,128)(2,1)S(1)}, bf16[256,512]{1,0:T(8,128)(2,1)S(1)}, u32[]{:S(2)}, u32[]{:S(2)}) collective-permute-start(bf16[256,512]{1,0:T(8,128)(2,1)S(1)} %fusion.65), channel_id=1, source_target_pairs={{0,6},{2,4},{4,2},{6,0},{1,7},{3,5},{5,3},{7,1},{8,14},{10,12},{12... | collective-permute-start | bytes 786440 | tf_op jit(solution)/shard_map/ppermute | solution.py:54
  41.1 10.3 %collective-permute-start.5 = (bf16[256,512]{1,0:T(8,128)(2,1)S(1)}, bf16[256,512]{1,0:T(8,128)(2,1)S(1)}, u32[]{:S(2)}, u32[]{:S(2)}) collective-permute-start(bf16[256,512]{1,0:T(8,128)(2,1)S(1)} %fusion.65), channel_id=1, source_target_pairs={{0,4},{2,6},{4,0},{6,2},{1,5},{3,7},{5,1},{7,3},{8,12},{10,14},{12... | collective-permute-start | bytes 786440 | tf_op jit(solution)/shard_map/ppermute | solution.py:54
  45.9 7.6 %collective-permute-start.3 = (bf16[256,512]{1,0:T(8,128)(2,1)S(1)}, bf16[256,512]{1,0:T(8,128)(2,1)S(1)}, u32[]{:S(2)}, u32[]{:S(2)}) collective-permute-start(bf16[256,512]{1,0:T(8,128)(2,1)S(1)} %fusion.65), channel_id=1, source_target_pairs={{0,2},{2,0},{4,6},{6,4},{1,3},{3,1},{5,7},{7,5},{8,10},{10,8},{12,... | collective-permute-start | bytes 786440 | tf_op jit(solution)/shard_map/ppermute | solution.py:54
  51.4 8.3 %collective-permute-start.1 = (bf16[256,512]{1,0:T(8,128)(2,1)S(1)}, bf16[256,512]{1,0:T(8,128)(2,1)S(1)}, u32[]{:S(2)}, u32[]{:S(2)}) collective-permute-start(bf16[256,512]{1,0:T(8,128)(2,1)S(1)} %fusion.65), channel_id=1, source_target_pairs={{0,1},{1,0},{2,3},{3,2},{4,5},{5,4},{6,7},{7,6},{8,9},{9,8},{10,11... | collective-permute-start | bytes 786440 | tf_op jit(solution)/shard_map/ppermute | solution.py:49
  77.3 10.1 %collective-permute-start.10 = (bf16[256,512]{1,0:T(8,128)(2,1)S(1)}, bf16[256,512]{1,0:T(8,128)(2,1)S(1)}, u32[]{:S(2)}, u32[]{:S(2)}) collective-permute-start(bf16[256,512]{1,0:T(8,128)(2,1)S(1)} %fusion.21), channel_id=1, source_target_pairs={{0,6},{2,4},{4,2},{6,0},{1,7},{3,5},{5,3},{7,1},{8,14},{10,12},{12... | collective-permute-start | bytes 786440 | tf_op jit(solution)/shard_map/ppermute | solution.py:54
  80.0 12.5 %collective-permute-start.11 = (bf16[256,512]{1,0:T(8,128)(2,1)S(1)}, bf16[256,512]{1,0:T(8,128)(2,1)S(1)}, u32[]{:S(2)}, u32[]{:S(2)}) collective-permute-start(bf16[256,512]{1,0:T(8,128)(2,1)S(1)} %fusion.22), channel_id=1, source_target_pairs={{0,2},{2,0},{4,6},{6,4},{1,3},{3,1},{5,7},{7,5},{8,10},{10,8},{12,... | collective-permute-start | bytes 786440 | tf_op jit(solution)/shard_map/ppermute | solution.py:54
  80.8 11.7 %collective-permute-start.12 = (bf16[256,512]{1,0:T(8,128)(2,1)S(1)}, bf16[256,512]{1,0:T(8,128)(2,1)S(1)}, u32[]{:S(2)}, u32[]{:S(2)}) collective-permute-start(bf16[256,512]{1,0:T(8,128)(2,1)S(1)} %fusion.23), channel_id=1, source_target_pairs={{0,4},{2,6},{4,0},{6,2},{1,5},{3,7},{5,1},{7,3},{8,12},{10,14},{12... | collective-permute-start | bytes 786440 | tf_op jit(solution)/shard_map/ppermute | solution.py:54
  87.5 37.6 %collective-permute-start.36 = (bf16[256,256]{1,0:T(8,128)(2,1)S(1)}, bf16[256,256]{1,0:T(8,128)(2,1)S(1)}, u32[]{:S(2)}, u32[]{:S(2)}) collective-permute-start(bf16[256,256]{1,0:T(8,128)(2,1)S(1)} %copy-done.34), channel_id=1, source_target_pairs={{0,1},{1,0},{2,3},{3,2},{4,5},{5,4},{6,7},{7,6},{8,9},{9,8},{10,11... | collective-permute-start | bytes 393224 | tf_op jit(solution)/shard_map/ppermute | solution.py:49
  92.4 28.8 %collective-permute-start.32 = (bf16[256,256]{1,0:T(8,128)(2,1)S(1)}, bf16[256,256]{1,0:T(8,128)(2,1)S(1)}, u32[]{:S(2)}, u32[]{:S(2)}) collective-permute-start(bf16[256,256]{1,0:T(8,128)(2,1)S(1)} %copy-done.35), channel_id=1, source_target_pairs={{0,1},{1,0},{2,3},{3,2},{4,5},{5,4},{6,7},{7,6},{8,9},{9,8},{10,11... | collective-permute-start | bytes 393224 | tf_op jit(solution)/shard_map/ppermute | solution.py:49
  96.1 32.8 %collective-permute-start.40 = (bf16[256,256]{1,0:T(8,128)(2,1)S(1)}, bf16[256,256]{1,0:T(8,128)(2,1)S(1)}, u32[]{:S(2)}, u32[]{:S(2)}) collective-permute-start(bf16[256,256]{1,0:T(8,128)(2,1)S(1)} %fusion.36), channel_id=1, source_target_pairs={{0,1},{1,0},{2,3},{3,2},{4,5},{5,4},{6,7},{7,6},{8,9},{9,8},{10,11... | collective-permute-start | bytes 393224 | tf_op jit(solution)/shard_map/ppermute | solution.py:49
  96.5 15.7 %collective-permute-start.21 = (bf16[256,512]{1,0:T(8,128)(2,1)S(1)}, bf16[256,512]{1,0:T(8,128)(2,1)S(1)}, u32[]{:S(2)}, u32[]{:S(2)}) collective-permute-start(bf16[256,512]{1,0:T(8,128)(2,1)S(1)} %multiply_convert_fusion), channel_id=1, source_target_pairs={{0,2},{2,0},{4,6},{6,4},{1,3},{3,1},{5,7},{7,5},{8,10},{10,8},{12,... | collective-permute-start | bytes 786440 | tf_op jit(solution)/shard_map/ppermute | solution.py:54
  99.4 11.8 %collective-permute-start.17 = (bf16[256,512]{1,0:T(8,128)(2,1)S(1)}, bf16[256,512]{1,0:T(8,128)(2,1)S(1)}, u32[]{:S(2)}, u32[]{:S(2)}) collective-permute-start(bf16[256,512]{1,0:T(8,128)(2,1)S(1)} %multiply_convert_fusion), channel_id=1, source_target_pairs={{0,6},{2,4},{4,2},{6,0},{1,7},{3,5},{5,3},{7,1},{8,14},{10,12},{12... | collective-permute-start | bytes 786440 | tf_op jit(solution)/shard_map/ppermute | solution.py:54
  111.2 7.8 %collective-permute-start.25 = (bf16[256,512]{1,0:T(8,128)(2,1)S(1)}, bf16[256,512]{1,0:T(8,128)(2,1)S(1)}, u32[]{:S(2)}, u32[]{:S(2)}) collective-permute-start(bf16[256,512]{1,0:T(8,128)(2,1)S(1)} %multiply_convert_fusion), channel_id=1, source_target_pairs={{0,4},{2,6},{4,0},{6,2},{1,5},{3,7},{5,1},{7,3},{8,12},{10,14},{12... | collective-permute-start | bytes 786440 | tf_op jit(solution)/shard_map/ppermute | solution.py:54
  112.3 7.0 %collective-permute-start.18 = (bf16[256,512]{1,0:T(8,128)(2,1)S(1)}, bf16[256,512]{1,0:T(8,128)(2,1)S(1)}, u32[]{:S(2)}, u32[]{:S(2)}) collective-permute-start(bf16[256,512]{1,0:T(8,128)(2,1)S(1)} %collective-permute-done.17), channel_id=1, source_target_pairs={{0,1},{1,0},{2,3},{3,2},{4,5},{5,4},{6,7},{7,6},{8,9},{9,8},{10,11... | collective-permute-start | bytes 786440 | tf_op jit(solution)/shard_map/ppermute | solution.py:49
  119.0 13.9 %collective-permute-start.16 = (bf16[256,256]{1,0:T(8,128)(2,1)S(1)}, bf16[256,256]{1,0:T(8,128)(2,1)S(1)}, u32[]{:S(2)}, u32[]{:S(2)}) collective-permute-start(bf16[256,256]{1,0:T(8,128)(2,1)S(1)} %get-tuple-element.120), channel_id=1, source_target_pairs={{0,1},{1,0},{2,3},{3,2},{4,5},{5,4},{6,7},{7,6},{8,9},{9,8},{10,11... | collective-permute-start | bytes 393224 | tf_op jit(solution)/shard_map/ppermute | solution.py:49
  121.2 19.4 %collective-permute-start.30 = (bf16[256,512]{1,0:T(8,128)(2,1)S(1)}, bf16[256,512]{1,0:T(8,128)(2,1)S(1)}, u32[]{:S(2)}, u32[]{:S(2)}) collective-permute-start(bf16[256,512]{1,0:T(8,128)(2,1)S(1)} %pad_maximum_fusion.9), channel_id=1, source_target_pairs={{0,1},{1,0},{2,3},{3,2},{4,5},{5,4},{6,7},{7,6},{8,9},{9,8},{10,11... | collective-permute-start | bytes 786440 | tf_op jit(solution)/shard_map/ppermute | solution.py:49
  125.1 7.1 %collective-permute-start.19 = (bf16[256,256]{1,0:T(8,128)(2,1)S(1)}, bf16[256,256]{1,0:T(8,128)(2,1)S(1)}, u32[]{:S(2)}, u32[]{:S(2)}) collective-permute-start(bf16[256,256]{1,0:T(8,128)(2,1)S(1)} %get-tuple-element.117), channel_id=1, source_target_pairs={{0,1},{1,0},{2,3},{3,2},{4,5},{5,4},{6,7},{7,6},{8,9},{9,8},{10,11... | collective-permute-start | bytes 393224 | tf_op jit(solution)/shard_map/ppermute | solution.py:49
  126.7 6.3 %collective-permute-start.23 = (bf16[256,256]{1,0:T(8,128)(2,1)S(1)}, bf16[256,256]{1,0:T(8,128)(2,1)S(1)}, u32[]{:S(2)}, u32[]{:S(2)}) collective-permute-start(bf16[256,256]{1,0:T(8,128)(2,1)S(1)} %get-tuple-element.118), channel_id=1, source_target_pairs={{0,1},{1,0},{2,3},{3,2},{4,5},{5,4},{6,7},{7,6},{8,9},{9,8},{10,11... | collective-permute-start | bytes 393224 | tf_op jit(solution)/shard_map/ppermute | solution.py:49
  133.0 6.7 %collective-permute-start.41 = (bf16[256,512]{1,0:T(8,128)(2,1)S(1)}, bf16[256,512]{1,0:T(8,128)(2,1)S(1)}, u32[]{:S(2)}, u32[]{:S(2)}) collective-permute-start(bf16[256,512]{1,0:T(8,128)(2,1)S(1)} %pad_maximum_fusion.12), channel_id=1, source_target_pairs={{0,1},{1,0},{2,3},{3,2},{4,5},{5,4},{6,7},{7,6},{8,9},{9,8},{10,11... | collective-permute-start | bytes 786440 | tf_op jit(solution)/shard_map/ppermute | solution.py:49
  133.5 31.4 %collective-permute-start.20 = (bf16[256,512]{1,0:T(8,128)(2,1)S(1)}, bf16[256,512]{1,0:T(8,128)(2,1)S(1)}, u32[]{:S(2)}, u32[]{:S(2)}) collective-permute-start(bf16[256,512]{1,0:T(8,128)(2,1)S(1)} %fusion.24), channel_id=1, source_target_pairs={{0,6},{2,4},{4,2},{6,0},{1,7},{3,5},{5,3},{7,1},{8,14},{10,12},{12... | collective-permute-start | bytes 786440 | tf_op jit(solution)/shard_map/ppermute | solution.py:54
  135.9 29.0 %collective-permute-start.24 = (bf16[256,512]{1,0:T(8,128)(2,1)S(1)}, bf16[256,512]{1,0:T(8,128)(2,1)S(1)}, u32[]{:S(2)}, u32[]{:S(2)}) collective-permute-start(bf16[256,512]{1,0:T(8,128)(2,1)S(1)} %fusion.25), channel_id=1, source_target_pairs={{0,2},{2,0},{4,6},{6,4},{1,3},{3,1},{5,7},{7,5},{8,10},{10,8},{12,... | collective-permute-start | bytes 786440 | tf_op jit(solution)/shard_map/ppermute | solution.py:54
  136.8 18.0 %collective-permute-start.34 = (bf16[256,512]{1,0:T(8,128)(2,1)S(1)}, bf16[256,512]{1,0:T(8,128)(2,1)S(1)}, u32[]{:S(2)}, u32[]{:S(2)}) collective-permute-start(bf16[256,512]{1,0:T(8,128)(2,1)S(1)} %fusion.18), channel_id=1, source_target_pairs={{0,6},{2,4},{4,2},{6,0},{1,7},{3,5},{5,3},{7,1},{8,14},{10,12},{12... | collective-permute-start | bytes 786440 | tf_op jit(solution)/shard_map/ppermute | solution.py:54
  139.7 19.0 %collective-permute-start.38 = (bf16[256,512]{1,0:T(8,128)(2,1)S(1)}, bf16[256,512]{1,0:T(8,128)(2,1)S(1)}, u32[]{:S(2)}, u32[]{:S(2)}) collective-permute-start(bf16[256,512]{1,0:T(8,128)(2,1)S(1)} %fusion.19), channel_id=1, source_target_pairs={{0,2},{2,0},{4,6},{6,4},{1,3},{3,1},{5,7},{7,5},{8,10},{10,8},{12,... | collective-permute-start | bytes 786440 | tf_op jit(solution)/shard_map/ppermute | solution.py:54
  140.6 18.0 %collective-permute-start.42 = (bf16[256,512]{1,0:T(8,128)(2,1)S(1)}, bf16[256,512]{1,0:T(8,128)(2,1)S(1)}, u32[]{:S(2)}, u32[]{:S(2)}) collective-permute-start(bf16[256,512]{1,0:T(8,128)(2,1)S(1)} %fusion.20), channel_id=1, source_target_pairs={{0,4},{2,6},{4,0},{6,2},{1,5},{3,7},{5,1},{7,3},{8,12},{10,14},{12... | collective-permute-start | bytes 786440 | tf_op jit(solution)/shard_map/ppermute | solution.py:54
  154.8 10.1 %collective-permute-start.28 = (bf16[256,512]{1,0:T(8,128)(2,1)S(1)}, bf16[256,512]{1,0:T(8,128)(2,1)S(1)}, u32[]{:S(2)}, u32[]{:S(2)}) collective-permute-start(bf16[256,512]{1,0:T(8,128)(2,1)S(1)} %fusion.26), channel_id=1, source_target_pairs={{0,4},{2,6},{4,0},{6,2},{1,5},{3,7},{5,1},{7,3},{8,12},{10,14},{12... | collective-permute-start | bytes 786440 | tf_op jit(solution)/shard_map/ppermute | solution.py:54
  160.3 63.4 %collective-permute-start.81 = (bf16[256,1536]{1,0:T(8,128)(2,1)}, bf16[256,1536]{1,0:T(8,128)(2,1)}, u32[]{:S(2)}, u32[]{:S(2)}) collective-permute-start(bf16[256,1536]{1,0:T(8,128)(2,1)} %constant_dynamic-slice_fusion.1), channel_id=1, source_target_pairs={{0,8},{8,0},{16,24},{24,16},{1,9},{9,1},{17,25},{25,17},{2,10},{10... | collective-permute-start | bytes 2359304 | tf_op jit(solution)/shard_map/ppermute | solution.py:54
  162.1 10.1 %collective-permute-start.49 = (bf16[256,512]{1,0:T(8,128)(2,1)S(1)}, bf16[256,512]{1,0:T(8,128)(2,1)S(1)}, u32[]{:S(2)}, u32[]{:S(2)}) collective-permute-start(bf16[256,512]{1,0:T(8,128)(2,1)S(1)} %fusion.209), channel_id=1, source_target_pairs={{0,6},{2,4},{4,2},{6,0},{1,7},{3,5},{5,3},{7,1},{8,14},{10,12},{12... | collective-permute-start | bytes 786440 | tf_op jit(solution)/shard_map/ppermute | solution.py:54
  166.1 11.0 %collective-permute-start.47 = (bf16[256,512]{1,0:T(8,128)(2,1)S(1)}, bf16[256,512]{1,0:T(8,128)(2,1)S(1)}, u32[]{:S(2)}, u32[]{:S(2)}) collective-permute-start(bf16[256,512]{1,0:T(8,128)(2,1)S(1)} %fusion.209), channel_id=1, source_target_pairs={{0,4},{2,6},{4,0},{6,2},{1,5},{3,7},{5,1},{7,3},{8,12},{10,14},{12... | collective-permute-start | bytes 786440 | tf_op jit(solution)/shard_map/ppermute | solution.py:54
  166.6 11.0 %collective-permute-start.45 = (bf16[256,512]{1,0:T(8,128)(2,1)S(1)}, bf16[256,512]{1,0:T(8,128)(2,1)S(1)}, u32[]{:S(2)}, u32[]{:S(2)}) collective-permute-start(bf16[256,512]{1,0:T(8,128)(2,1)S(1)} %fusion.209), channel_id=1, source_target_pairs={{0,2},{2,0},{4,6},{6,4},{1,3},{3,1},{5,7},{7,5},{8,10},{10,8},{12,... | collective-permute-start | bytes 786440 | tf_op jit(solution)/shard_map/ppermute | solution.py:54
  172.5 8.3 %collective-permute-start.50 = (bf16[256,256]{1,0:T(8,128)(2,1)S(1)}, bf16[256,256]{1,0:T(8,128)(2,1)S(1)}, u32[]{:S(2)}, u32[]{:S(2)}) collective-permute-start(bf16[256,256]{1,0:T(8,128)(2,1)S(1)} %convolution_convert_fusion.6), channel_id=1, source_target_pairs={{0,1},{1,0},{2,3},{3,2},{4,5},{5,4},{6,7},{7,6},{8,9},{9,8},{10,11... | collective-permute-start | bytes 393224 | tf_op jit(solution)/shard_map/ppermute | solution.py:49
  180.4 47.9 %collective-permute-start.77 = (bf16[256,512]{1,0:T(8,128)(2,1)}, bf16[256,512]{1,0:T(8,128)(2,1)}, u32[]{:S(2)}, u32[]{:S(2)}) collective-permute-start(bf16[256,512]{1,0:T(8,128)(2,1)} %fusion.100), channel_id=1, source_target_pairs={{0,8},{8,0},{16,24},{24,16},{1,9},{9,1},{17,25},{25,17},{2,10},{10... | collective-permute-start | bytes 786440 | tf_op jit(solution)/shard_map/ppermute | solution.py:54
  210.4 8.6 %collective-permute-start.56 = (f32[8,512]{1,0:T(8,128)}, f32[8,512]{1,0:T(8,128)S(1)}, u32[]{:S(2)}, u32[]{:S(2)}) collective-permute-start(f32[8,512]{1,0:T(8,128)} %get-tuple-element.33), channel_id=1, source_target_pairs={{0,8},{8,0},{16,24},{24,16},{1,9},{9,1},{17,25},{25,17},{2,10},{10... | collective-permute-start | bytes 49160 | tf_op jit(solution)/shard_map/ppermute | solution.py:54
  223.1 81.3 %collective-permute-start.51 = (bf16[4,256,896]{2,1,0:T(8,128)(2,1)}, bf16[4,256,896]{2,1,0:T(8,128)(2,1)}, u32[]{:S(2)}, u32[]{:S(2)}) collective-permute-start(bf16[4,256,896]{2,1,0:T(8,128)(2,1)} %get-tuple-element.32), channel_id=1, source_target_pairs={{0,1},{1,0},{2,3},{3,2},{4,5},{5,4},{6,7},{7,6},{8,9},{9,8},{10,11... | collective-permute-start | bytes 5505032 | tf_op jit(solution)/shard_map/ppermute | solution.py:49
  225.1 23.2 %collective-permute-start.82 = (bf16[128,1536]{1,0:T(8,128)(2,1)S(1)}, bf16[128,1536]{1,0:T(8,128)(2,1)S(1)}, u32[]{:S(2)}, u32[]{:S(2)}) collective-permute-start(bf16[128,1536]{1,0:T(8,128)(2,1)S(1)} %constant_dynamic-slice_fusion), channel_id=1, source_target_pairs={{0,16},{8,24},{16,0},{24,8},{1,17},{9,25},{17,1},{25,9},{2,18},{10... | collective-permute-start | bytes 1179656 | tf_op jit(solution)/shard_map/ppermute | solution.py:54
  228.3 48.8 %collective-permute-start.58 = (f32[8,512]{1,0:T(8,128)S(1)}, f32[8,512]{1,0:T(8,128)S(1)}, u32[]{:S(2)}, u32[]{:S(2)}) collective-permute-start(f32[8,512]{1,0:T(8,128)S(1)} %pad.168), channel_id=1, source_target_pairs={{0,1},{1,0},{2,3},{3,2},{4,5},{5,4},{6,7},{7,6},{8,9},{9,8},{10,11... | collective-permute-start | bytes 49160 | tf_op jit(solution)/shard_map/ppermute | solution.py:49
  229.7 32.7 %collective-permute-start.78 = (bf16[128,512]{1,0:T(8,128)(2,1)S(1)}, bf16[128,512]{1,0:T(8,128)(2,1)S(1)}, u32[]{:S(2)}, u32[]{:S(2)}) collective-permute-start(bf16[128,512]{1,0:T(8,128)(2,1)S(1)} %constant_dynamic-slice_fusion.2), channel_id=1, source_target_pairs={{0,16},{8,24},{16,0},{24,8},{1,17},{9,25},{17,1},{25,9},{2,18},{10... | collective-permute-start | bytes 393224 | tf_op jit(solution)/shard_map/ppermute | solution.py:54
  248.4 25.2 %collective-permute-start.83 = (bf16[128,1536]{1,0:T(8,128)(2,1)S(1)}, bf16[128,1536]{1,0:T(8,128)(2,1)S(1)}, u32[]{:S(2)}, u32[]{:S(2)}) collective-permute-start(bf16[128,1536]{1,0:T(8,128)(2,1)S(1)} %add_convert_fusion.2), channel_id=1, source_target_pairs={{0,16},{8,24},{16,0},{24,8},{1,17},{9,25},{17,1},{25,9},{2,18},{10... | collective-permute-start | bytes 1179656 | tf_op jit(solution)/shard_map/ppermute | solution.py:54
  262.4 11.1 %collective-permute-start.79 = (bf16[128,512]{1,0:T(8,128)(2,1)S(1)}, bf16[128,512]{1,0:T(8,128)(2,1)S(1)}, u32[]{:S(2)}, u32[]{:S(2)}) collective-permute-start(bf16[128,512]{1,0:T(8,128)(2,1)S(1)} %add_convert_fusion.5), channel_id=1, source_target_pairs={{0,16},{8,24},{16,0},{24,8},{1,17},{9,25},{17,1},{25,9},{2,18},{10... | collective-permute-start | bytes 393224 | tf_op jit(solution)/shard_map/ppermute | solution.py:54
  273.5 9.2 %collective-permute-start.80 = (bf16[256,512]{1,0:T(8,128)(2,1)S(1)}, bf16[256,512]{1,0:T(8,128)(2,1)S(1)}, u32[]{:S(2)}, u32[]{:S(2)}) collective-permute-start(bf16[256,512]{1,0:T(8,128)(2,1)S(1)} %maximum_select_fusion.11), channel_id=1, source_target_pairs={{0,8},{8,0},{16,24},{24,16},{1,9},{9,1},{17,25},{25,17},{2,10},{10... | collective-permute-start | bytes 786440 | tf_op jit(solution)/shard_map/ppermute | solution.py:54
  273.8 25.0 %collective-permute-start.84 = (bf16[256,1536]{1,0:T(8,128)(2,1)S(1)}, bf16[256,1536]{1,0:T(8,128)(2,1)}, u32[]{:S(2)}, u32[]{:S(2)}) collective-permute-start(bf16[256,1536]{1,0:T(8,128)(2,1)S(1)} %maximum_select_fusion.7), channel_id=1, source_target_pairs={{0,8},{8,0},{16,24},{24,16},{1,9},{9,1},{17,25},{25,17},{2,10},{10... | collective-permute-start | bytes 2359304 | tf_op jit(solution)/shard_map/ppermute | solution.py:54
  306.0 25.5 %collective-permute-start.52 = (bf16[256,512]{1,0:T(8,128)(2,1)S(1)}, bf16[256,512]{1,0:T(8,128)(2,1)S(1)}, u32[]{:S(2)}, u32[]{:S(2)}) collective-permute-start(bf16[256,512]{1,0:T(8,128)(2,1)S(1)} %fusion.15), channel_id=1, source_target_pairs={{0,6},{2,4},{4,2},{6,0},{1,7},{3,5},{5,3},{7,1},{8,14},{10,12},{12... | collective-permute-start | bytes 786440 | tf_op jit(solution)/shard_map/ppermute | solution.py:54
  309.9 21.5 %collective-permute-start.53 = (bf16[256,512]{1,0:T(8,128)(2,1)S(1)}, bf16[256,512]{1,0:T(8,128)(2,1)S(1)}, u32[]{:S(2)}, u32[]{:S(2)}) collective-permute-start(bf16[256,512]{1,0:T(8,128)(2,1)S(1)} %fusion.16), channel_id=1, source_target_pairs={{0,2},{2,0},{4,6},{6,4},{1,3},{3,1},{5,7},{7,5},{8,10},{10,8},{12,... | collective-permute-start | bytes 786440 | tf_op jit(solution)/shard_map/ppermute | solution.py:54
  316.4 7.7 %collective-permute-start.67 = (bf16[128,512]{1,0:T(8,128)(2,1)S(1)}, bf16[128,512]{1,0:T(8,128)(2,1)S(1)}, u32[]{:S(2)}, u32[]{:S(2)}) collective-permute-start(bf16[128,512]{1,0:T(8,128)(2,1)S(1)} %get-tuple-element.114), channel_id=1, source_target_pairs={{0,6},{2,4},{4,2},{6,0},{1,7},{3,5},{5,3},{7,1},{8,14},{10,12},{12... | collective-permute-start | bytes 393224 | tf_op jit(solution)/shard_map/ppermute | solution.py:54
  317.9 7.9 %collective-permute-start.69 = (bf16[128,512]{1,0:T(8,128)(2,1)S(1)}, bf16[128,512]{1,0:T(8,128)(2,1)S(1)}, u32[]{:S(2)}, u32[]{:S(2)}) collective-permute-start(bf16[128,512]{1,0:T(8,128)(2,1)S(1)} %get-tuple-element.115), channel_id=1, source_target_pairs={{0,4},{2,6},{4,0},{6,2},{1,5},{3,7},{5,1},{7,3},{8,12},{10,14},{12... | collective-permute-start | bytes 393224 | tf_op jit(solution)/shard_map/ppermute | solution.py:54
  319.4 6.4 %collective-permute-start.68 = (bf16[128,512]{1,0:T(8,128)(2,1)S(1)}, bf16[128,512]{1,0:T(8,128)(2,1)S(1)}, u32[]{:S(2)}, u32[]{:S(2)}) collective-permute-start(bf16[128,512]{1,0:T(8,128)(2,1)S(1)} %get-tuple-element.116), channel_id=1, source_target_pairs={{0,2},{2,0},{4,6},{6,4},{1,3},{3,1},{5,7},{7,5},{8,10},{10,8},{12,... | collective-permute-start | bytes 393224 | tf_op jit(solution)/shard_map/ppermute | solution.py:54
  324.1 7.4 %collective-permute-start.54 = (bf16[256,512]{1,0:T(8,128)(2,1)S(1)}, bf16[256,512]{1,0:T(8,128)(2,1)S(1)}, u32[]{:S(2)}, u32[]{:S(2)}) collective-permute-start(bf16[256,512]{1,0:T(8,128)(2,1)S(1)} %fusion.17), channel_id=1, source_target_pairs={{0,4},{2,6},{4,0},{6,2},{1,5},{3,7},{5,1},{7,3},{8,12},{10,14},{12... | collective-permute-start | bytes 786440 | tf_op jit(solution)/shard_map/ppermute | solution.py:54
  326.7 27.8 %collective-permute-start.63 = (bf16[256,1024]{1,0:T(8,128)(2,1)S(1)}, bf16[256,1024]{1,0:T(8,128)(2,1)S(1)}, u32[]{:S(2)}, u32[]{:S(2)}) collective-permute-start(bf16[256,1024]{1,0:T(8,128)(2,1)S(1)} %fusion.71), channel_id=1, source_target_pairs={{0,8},{8,0},{16,24},{24,16},{1,9},{9,1},{17,25},{25,17},{2,10},{10... | collective-permute-start | bytes 1572872 | tf_op jit(solution)/shard_map/ppermute | solution.py:54
  331.4 7.3 %collective-permute-start.71 = (bf16[32,512]{1,0:T(8,128)(2,1)S(1)}, bf16[32,512]{1,0:T(8,128)(2,1)S(1)}, u32[]{:S(2)}, u32[]{:S(2)}) collective-permute-start(bf16[32,512]{1,0:T(8,128)(2,1)S(1)} %constant_dynamic-slice_fusion.3), channel_id=1, source_target_pairs={{0,16},{8,24},{16,0},{24,8},{1,17},{9,25},{17,1},{25,9},{2,18},{10... | collective-permute-start | bytes 98312 | tf_op jit(solution)/shard_map/ppermute | solution.py:54
  333.3 8.9 %collective-permute-start.59 = (f32[2,512]{1,0:T(2,128)S(1)}, f32[2,512]{1,0:T(2,128)S(1)}, u32[]{:S(2)}, u32[]{:S(2)}) collective-permute-start(f32[2,512]{1,0:T(2,128)S(1)} %pad_maximum_fusion.22), channel_id=1, source_target_pairs={{0,8},{8,0},{16,24},{24,16},{1,9},{9,1},{17,25},{25,17},{2,10},{10... | collective-permute-start | bytes 12296 | tf_op jit(solution)/shard_map/ppermute | solution.py:54
  342.2 6.1 %collective-permute-start.55 = (f32[256]{0:T(256)S(1)}, f32[256]{0:T(256)S(1)}, u32[]{:S(2)}, u32[]{:S(2)}) collective-permute-start(f32[256]{0:T(256)S(1)} %get-tuple-element.81), channel_id=1, source_target_pairs={{0,1},{1,0},{2,3},{3,2},{4,5},{5,4},{6,7},{7,6},{8,9},{9,8},{10,11... | collective-permute-start | bytes 3080 | tf_op jit(solution)/shard_map/ppermute | solution.py:49
  344.2 11.8 %collective-permute-start.73 = (bf16[64,512]{1,0:T(8,128)(2,1)S(1)}, bf16[64,512]{1,0:T(8,128)(2,1)S(1)}, u32[]{:S(2)}, u32[]{:S(2)}) collective-permute-start(bf16[64,512]{1,0:T(8,128)(2,1)S(1)} %maximum_select_fusion.13), channel_id=1, source_target_pairs={{0,8},{8,0},{16,24},{24,16},{1,9},{9,1},{17,25},{25,17},{2,10},{10... | collective-permute-start | bytes 196616 | tf_op jit(solution)/shard_map/ppermute | solution.py:54
  354.7 10.0 %collective-permute-start.64 = (bf16[128,1024]{1,0:T(8,128)(2,1)S(1)}, bf16[128,1024]{1,0:T(8,128)(2,1)S(1)}, u32[]{:S(2)}, u32[]{:S(2)}) collective-permute-start(bf16[128,1024]{1,0:T(8,128)(2,1)S(1)} %constant_dynamic-slice_fusion.8), channel_id=1, source_target_pairs={{0,16},{8,24},{16,0},{24,8},{1,17},{9,25},{17,1},{25,9},{2,18},{10... | collective-permute-start | bytes 786440 | tf_op jit(solution)/shard_map/ppermute | solution.py:54
  356.1 11.9 %collective-permute-start.75 = (bf16[128,512]{1,0:T(8,128)(2,1)S(1)}, bf16[128,512]{1,0:T(8,128)(2,1)S(1)}, u32[]{:S(2)}, u32[]{:S(2)}) collective-permute-start(bf16[128,512]{1,0:T(8,128)(2,1)S(1)} %get-tuple-element.83), channel_id=1, source_target_pairs={{0,4},{2,6},{4,0},{6,2},{1,5},{3,7},{5,1},{7,3},{8,12},{10,14},{12... | collective-permute-start | bytes 393224 | tf_op jit(solution)/shard_map/ppermute | solution.py:54
  357.2 10.8 %collective-permute-start.74 = (bf16[128,512]{1,0:T(8,128)(2,1)S(1)}, bf16[128,512]{1,0:T(8,128)(2,1)S(1)}, u32[]{:S(2)}, u32[]{:S(2)}) collective-permute-start(bf16[128,512]{1,0:T(8,128)(2,1)S(1)} %get-tuple-element.83), channel_id=1, source_target_pairs={{0,2},{2,0},{4,6},{6,4},{1,3},{3,1},{5,7},{7,5},{8,10},{10,8},{12,... | collective-permute-start | bytes 393224 | tf_op jit(solution)/shard_map/ppermute | solution.py:54
  364.7 12.4 %collective-permute-start.65 = (bf16[128,1024]{1,0:T(8,128)(2,1)S(1)}, bf16[128,1024]{1,0:T(8,128)(2,1)S(1)}, u32[]{:S(2)}, u32[]{:S(2)}) collective-permute-start(bf16[128,1024]{1,0:T(8,128)(2,1)S(1)} %add_convert_fusion.4), channel_id=1, source_target_pairs={{0,16},{8,24},{16,0},{24,8},{1,17},{9,25},{17,1},{25,9},{2,18},{10... | collective-permute-start | bytes 786440 | tf_op jit(solution)/shard_map/ppermute | solution.py:54
  366.0 11.4 %collective-permute-start.76 = (bf16[128,512]{1,0:T(8,128)(2,1)S(1)}, bf16[128,512]{1,0:T(8,128)(2,1)S(1)}, u32[]{:S(2)}, u32[]{:S(2)}) collective-permute-start(bf16[128,512]{1,0:T(8,128)(2,1)S(1)} %get-tuple-element.83), channel_id=1, source_target_pairs={{0,6},{2,4},{4,2},{6,0},{1,7},{3,5},{5,3},{7,1},{8,14},{10,12},{12... | collective-permute-start | bytes 393224 | tf_op jit(solution)/shard_map/ppermute | solution.py:54
  377.3 13.9 %collective-permute-start.66 = (bf16[256,1024]{1,0:T(8,128)(2,1)S(1)}, bf16[256,1024]{1,0:T(8,128)(2,1)S(1)}, u32[]{:S(2)}, u32[]{:S(2)}) collective-permute-start(bf16[256,1024]{1,0:T(8,128)(2,1)S(1)} %maximum_select_fusion.8), channel_id=1, source_target_pairs={{0,8},{8,0},{16,24},{24,16},{1,9},{9,1},{17,25},{25,17},{2,10},{10... | collective-permute-start | bytes 1572872 | tf_op jit(solution)/shard_map/ppermute | solution.py:54
  (62 other events, 414.2 us)
